TPU v7x, 256 devices: a whole 4x4x8 slice. The times are simulated.
256 devices in a mesh: section: 8 (over y, x_hi), dp: 32 (over z, x_lo, core).
Axes of the slice: x: 4 (x_hi: 2, x_lo: 2; x = x_hi * 2 + x_lo), y: 4, z: 8, core: 2. Of those that a mesh axis runs over, the one named last changes fastest.
Arguments:
- clips: bfloat16 [64, 14, 8, 640], P('dp'), may hold values from -6 to 6
- cotangent: bfloat16 [64, 14, 8, 640], P('dp'), may hold values from -6 to 6
- timesteps: int32 [64], P('dp'), may hold values from 0 to 999
- time_table: bfloat16 [8, 1000, 640], P('section'), may hold values from -3 to 3
- skip_weights: bfloat16 [8, 640, 640], P('section'), may hold values from -0.125 to 0.125
- conv_weights: bfloat16 [8, 1920, 640], P('section'), may hold values from -0.125 to 0.125
- gains: float32 [8, 640], P('section'), may hold values from 0.5 to 1.5
Outputs:
- grad_skip: float32 [8, 640, 640], P('section')
- grad_conv: float32 [8, 1920, 640], P('section')
- grad_gain: float32 [8, 640], P('section')
All inputs are finite; a program needn't handle non-finite values.
Results may differ from a plain program's by a relative error of at most 0.017.
Values may be sent and summed in bfloat16 or wider, within the bound.
No kernel may reach another device: no remote copies, remote signals or barrier semaphores. Data moves between devices by JAX's collectives and lax.ppermute only.
A program may use at most 64 MiB of HBM per device.

v0:
```python
import jax
import jax.numpy as jnp
from jax import lax
from jax.experimental import pallas as pl
from jax.experimental.pallas import tpu as pltpu
from jax.sharding import PartitionSpec as P

EPSILON = 1e-05
LOW = jnp.bfloat16
HIGH = jnp.float32
SMALL_BYTES = 12 * 2**20
BIG_BYTES = 32 * 2**20
CHUNK_PAD = 8
GAIN_ROWS = 16
PIECES = 2


def dot(left, right):
    return lax.dot_general(left, right, (((1,), (0,)), ((), ())), preferred_element_type=HIGH)


def dot_transposed(left, right):
    return lax.dot_general(left, right, (((1,), (1,)), ((), ())), preferred_element_type=HIGH)


def dot_outer(left, right):
    return lax.dot_general(left, right, (((0,), (0,)), ((), ())), preferred_element_type=HIGH)


def later(value, pixels):
    return jnp.concatenate([jnp.zeros_like(value[:pixels]), value[:-pixels]], axis=0)


def earlier(value, pixels):
    return jnp.concatenate([value[pixels:], jnp.zeros_like(value[:pixels])], axis=0)


def level_forward(x, s, weight_ref, level, vec_ref, pixels):
    gain = vec_ref[pl.ds(level, 1), :]
    embed = vec_ref[pl.ds(2 + level, 1), :]
    mixed = x.astype(HIGH) + dot(s, weight_ref[level, 0]) + embed
    inv_rms = lax.rsqrt(jnp.mean(mixed * mixed, axis=-1, keepdims=True) + EPSILON)
    unit = mixed * inv_rms
    normed = (unit * gain).astype(LOW)
    before = dot(normed, weight_ref[level, 1])
    middle = dot(normed, weight_ref[level, 2])
    after_tap = dot(normed, weight_ref[level, 3])
    conv_out = middle + later(before, pixels) + earlier(after_tap, pixels)
    sigmoid = jax.nn.sigmoid(conv_out)
    out = (mixed + conv_out * sigmoid).astype(LOW)
    return out, inv_rms, unit, normed, sigmoid * (1.0 + conv_out * (1.0 - sigmoid))


def encoder_kernel(pixels, x_ref, weight_ref, vec_ref, first_ref, second_ref):
    def step(level, carry):
        x = second_ref[...]
        first_ref[...] = x
        second_ref[...] = level_forward(x, x, weight_ref, level, vec_ref, pixels)[0]
        return carry

    second_ref[...] = x_ref[...]
    lax.fori_loop(0, 2, step, 0)


def turn_kernel(pixels, x_ref, skip_ref, weight_ref, vec_ref, out_ref):
    def step(level, carry):
        x = out_ref[...]
        s = jnp.where(level == 0, x, skip_ref[...])
        out_ref[...] = level_forward(x, s, weight_ref, level, vec_ref, pixels)[0]
        return carry

    out_ref[...] = x_ref[...]
    lax.fori_loop(0, 2, step, 0)


def states_kernel(pixels, pairs, where_ref, *refs):
    xs, refs = refs[:pairs], refs[pairs:]
    side_ref, skip_ref, weight_ref, vec_ref = refs[:4]
    inv_ref, unit_ref, slope_ref, own_ref, give_ref, x_ref = refs[4:]
    pair = where_ref[2]
    odd = where_ref[3]
    x = jnp.where(pair == 0, xs[0][...], jnp.zeros_like(xs[0]))
    for ref in xs[1:]:
        x = x + ref[...]
    rows = x.shape[0]
    x_ref[...] = x

    def step(level, carry):
        x = x_ref[...]
        direct = jnp.logical_or(
            pair < pairs // 2, jnp.logical_and(level == 0, pair < pairs - 1)
        )
        first = jnp.where(level == 0, side_ref[rows:], side_ref[:rows] + skip_ref[...])
        s = jnp.where(direct, x, first)
        out, inv_rms, unit, normed, slope = level_forward(x, s, weight_ref, level, vec_ref, pixels)
        x_ref[...] = out
        inv_ref[level] = jnp.broadcast_to(inv_rms, inv_ref.shape[1:])
        unit_ref[level] = unit
        slope_ref[level] = slope

        def put(ref):
            ref[:rows] = normed
            ref[rows:] = s

        pl.when(level == odd)(lambda: put(own_ref))
        pl.when(level != odd)(lambda: put(give_ref))
        return carry

    lax.fori_loop(0, 2, step, 0)


def level_backward(d, states, weight_ref, level, vec_ref, pixels):
    inv_ref, unit_ref, slope_ref = states
    inv_rms = inv_ref[level][:, :1]
    unit = unit_ref[level]
    conv_low = (d * slope_ref[level]).astype(LOW)
    first = dot_transposed(conv_low, weight_ref[level, 1])
    middle = dot_transposed(conv_low, weight_ref[level, 2])
    last = dot_transposed(conv_low, weight_ref[level, 3])
    normed_grad = middle + earlier(first, pixels) + later(last, pixels)
    scaled = normed_grad * vec_ref[pl.ds(level, 1), :]
    mixed_grad = d + inv_rms * (
        scaled - unit * jnp.mean(scaled * unit, axis=-1, keepdims=True)
    )
    return conv_low, normed_grad, mixed_grad, mixed_grad.astype(LOW)


def skip_back(mixed_low, weight_ref, level):
    return dot_transposed(mixed_low, weight_ref[level, 0])


def rounded(value):
    return value.astype(LOW).astype(HIGH)


def decoder_back_kernel(pixels, d_ref, *refs):
    states, (weight_ref, vec_ref, out_ref, side_ref) = refs[:3], refs[3:]
    out_ref[...] = d_ref[...]

    def step(i, carry):
        level = 1 - i
        _, _, _, mixed_low = level_backward(
            out_ref[...].astype(HIGH), states, weight_ref, level, vec_ref, pixels
        )
        out_ref[...] = mixed_low
        side_ref[i] = skip_back(mixed_low, weight_ref, level).astype(LOW)
        return carry

    lax.fori_loop(0, 2, step, 0)


def turn_back_kernel(pixels, d_ref, *refs):
    states, (weight_ref, vec_ref, out_ref, side_ref) = refs[:3], refs[3:]
    out_ref[...] = d_ref[...]

    def step(i, carry):
        level = 1 - i
        _, _, mixed_grad, mixed_low = level_backward(
            out_ref[...].astype(HIGH), states, weight_ref, level, vec_ref, pixels
        )
        skip_grad = skip_back(mixed_low, weight_ref, level)

        @pl.when(i == 0)
        def _():
            out_ref[...] = mixed_low
            side_ref[...] = skip_grad.astype(LOW)

        @pl.when(i == 1)
        def _():
            out_ref[...] = (mixed_grad + skip_grad).astype(LOW)

        return carry

    lax.fori_loop(0, 2, step, 0)


def encoder_back_kernel(pixels, d_ref, extra_ref, *refs):
    states, (weight_ref, vec_ref, out_ref) = refs[:3], refs[3:]
    out_ref[...] = d_ref[...]

    def step(i, carry):
        level = 1 - i
        d = out_ref[...].astype(HIGH)
        d = jnp.where(i == 1, d + extra_ref[...].astype(HIGH), d)
        _, _, mixed_grad, mixed_low = level_backward(d, states, weight_ref, level, vec_ref, pixels)
        out_ref[...] = (mixed_grad + skip_back(mixed_low, weight_ref, level)).astype(LOW)
        return carry

    lax.fori_loop(0, 2, step, 0)


def last_kernel(pixels, pairs, where_ref, *refs):
    ds, refs = refs[:pairs], refs[pairs:]
    side_ref, extra_ref, *refs = refs
    states, (weight_ref, vec_ref, own_ref, give_ref, d_ref) = refs[:3], refs[3:]
    pair = where_ref[2]
    odd = where_ref[3]
    rows = extra_ref.shape[0]
    d = jnp.where(pair == pairs - 1, ds[0][...], jnp.zeros_like(ds[0])).astype(HIGH)
    for ref in ds[1:]:
        d = d + ref[...].astype(HIGH)
    d_ref[...] = d + side_ref[1].astype(HIGH)

    def step(i, carry):
        level = 1 - i
        conv_low, normed_grad, mixed_grad, mixed_low = level_backward(
            d_ref[...], states, weight_ref, level, vec_ref, pixels
        )
        gain = jnp.sum(normed_grad * states[1][level], axis=0, keepdims=True)

        @pl.when(i == 0)
        def _():
            joined = mixed_grad + skip_back(mixed_low, weight_ref, level)
            back = rounded(jnp.where(pair < pairs // 2, joined, mixed_grad))
            d_ref[...] = back + side_ref[0].astype(HIGH) + extra_ref[...].astype(HIGH)

        def put(ref):
            ref[:rows] = conv_low
            ref[rows : 2 * rows] = mixed_low
            high = jnp.broadcast_to(gain.astype(LOW), (GAIN_ROWS, gain.shape[1]))
            low = jnp.broadcast_to((gain - rounded(gain)).astype(LOW), high.shape)
            line = lax.broadcasted_iota(jnp.int32, high.shape, 0)
            ref[2 * rows :] = jnp.where(line == 0, high.astype(HIGH), low.astype(HIGH)).astype(LOW)

        pl.when(level == odd)(lambda: put(own_ref))
        pl.when(level != odd)(lambda: put(give_ref))
        return carry

    lax.fori_loop(0, 2, step, 0)


def weight_kernel(pixels, ring, where_ref, own_ref, got_ref, first_ref, early_ref, keep_ref, give_ref, grad_ref, left_ref, right_ref):
    _, chunk, width = keep_ref.shape
    used = chunk - CHUNK_PAD
    rows = first_ref.shape[0] // 2
    for n, (saved_ref, ref) in enumerate(((first_ref, own_ref), (early_ref, got_ref))):
        here = slice(n * rows, (n + 1) * rows)
        left_ref[0, here] = saved_ref[rows:]
        left_ref[1, here] = saved_ref[:rows]
        conv_grad = ref[:rows].astype(HIGH)
        right_ref[0, here] = ref[rows : 2 * rows]
        right_ref[1, here] = earlier(conv_grad, pixels).astype(LOW)
        right_ref[2, here] = ref[:rows]
        right_ref[3, here] = later(conv_grad, pixels).astype(LOW)
    gain = jnp.zeros((1, width), HIGH)
    for ref in (own_ref, got_ref):
        tail = ref[2 * rows :].astype(HIGH)
        gain = gain + tail[:1] + tail[1:2]
    grad_ref[:, used:, :] = jnp.zeros((2 * ring, CHUNK_PAD, width), LOW)
    grad_ref[0, used:, :] = jnp.broadcast_to(gain, (CHUNK_PAD, width)).astype(LOW)

    def multiply(matrix, carry):
        value = dot_outer(left_ref[jnp.minimum(matrix, 1)], right_ref[matrix]).astype(LOW)
        each = width // used
        grad_ref[pl.ds(matrix * each, each), :used, :] = value.reshape(each, used, width)
        return carry

    lax.fori_loop(0, 4, multiply, 0)
    core = where_ref[0]
    z = where_ref[1]
    side = where_ref[5]
    steps = ring // 2
    for half in range(2):
        first = (side ^ half) * ring
        for n in range(steps):
            lower = first + lax.rem(z + steps + n, ring)
            upper = first + lax.rem(z + steps - 1 - n, ring)
            keep_ref[half * steps + n] = grad_ref[jnp.where(core == 0, lower, upper)]
            give_ref[half * steps + n] = grad_ref[jnp.where(core == 0, upper, lower)]


def gather_kernel(where_ref, *refs):
    pieces = refs[: 4 * PIECES]
    skip_ref, conv_ref, out_ref = refs[4 * PIECES :]
    odd = where_ref[3]
    place = where_ref[4]
    out_ref[odd, 0] = skip_ref[0]
    width = skip_ref.shape[1]
    for tap in range(3):
        out_ref[odd, tap + 1] = conv_ref[0, tap * width : (tap + 1) * width]
    size = width // PIECES
    for m in range(4):
        matrix = place ^ m
        for n in range(PIECES):
            out_ref[1 - odd, matrix, n * size : (n + 1) * size, :] = pieces[m * PIECES + n][...]


def finish_kernel(scale, ring, where_ref, *refs):
    skip_ref, conv_ref, gain_ref, all_ref = refs[-4:]
    steps = ring // 2
    own, crossed, beside = refs[:steps], refs[steps : 2 * steps], refs[2 * steps : -4]
    chunk, width = own[0].shape
    used = chunk - CHUNK_PAD
    core = where_ref[0]
    z = where_ref[1]
    side = where_ref[5]
    other = [(ref, 2 * n) for ref in beside for n in range(ref.shape[0] // 2)]
    for n in range(steps):
        lower = lax.rem(z + 1 + n, ring)
        upper = lax.rem(z + ring - 1 - n, ring) if n < steps - 1 else z
        here = jnp.where(core == 0, lower, upper)
        there = jnp.where(core == 0, upper, lower)
        ref, at = other[n]
        all_ref[side * ring + here] = own[n][...]
        all_ref[(1 - side) * ring + here] = crossed[n][...]
        all_ref[side * ring + there] = ref[at]
        all_ref[(1 - side) * ring + there] = ref[at + 1]
    each = width // used

    def place(target_ref, first):
        def step(c, carry):
            start = pl.multiple_of(c * used, used)
            target_ref[0, pl.ds(start, used), :] = all_ref[first + c, :used, :].astype(HIGH) * scale
            return carry

        return step

    lax.fori_loop(0, each, place(skip_ref, 0), 0)
    lax.fori_loop(0, 3 * each, place(conv_ref, each), 0)
    gain_ref[...] = all_ref[0, used : used + 1, :].astype(HIGH) * scale


def call(kernel, outs, *args, scratch=(), scalars=0, limit=SMALL_BYTES):
    specs = [pl.BlockSpec(memory_space=pltpu.SMEM)] * scalars + [
        pl.BlockSpec(memory_space=pltpu.VMEM)
    ] * (len(args) - scalars)
    return pl.pallas_call(
        kernel,
        out_shape=outs,
        in_specs=specs,
        scratch_shapes=scratch,
        compiler_params=pltpu.CompilerParams(vmem_limit_bytes=limit),
    )(*args)


def after(value, other):
    return lax.optimization_barrier((value, other))[0]


def make_local(sizes):
    sections = sizes["section"]
    dp = sizes["dp"]
    pairs = sections // 2
    cross = 2
    ring = dp // 4

    def local(clips, cotangent, timesteps, time_table, skip_weights, conv_weights, gains):
        both = ("section", "dp")
        section = lax.axis_index("section")
        member = lax.axis_index("dp")
        odd = section % 2
        where = jnp.stack(
            [member % 2, member // 4, section // 2, odd, member % 4, member // 2 % 2]
        ).astype(jnp.int32)
        count, frames, pixels, width = clips.shape
        rows = frames * pixels
        low = lambda *shape: jax.ShapeDtypeStruct(shape, LOW)
        high = lambda *shape: jax.ShapeDtypeStruct(shape, HIGH)

        def move(value, section_of, member_of, only=range(sections)):
            return lax.ppermute(
                value,
                both,
                [(s * dp + i, section_of(s) * dp + member_of(i)) for s in only for i in range(dp)],
            )

        same = lambda i: i
        to_core = lambda i: i ^ 1
        to_x = lambda i: i ^ cross
        partner = lambda s: s ^ 1

        def hop(value, source, target):
            return move(
                value, lambda s: s + 2 * (target - source), same, (2 * source, 2 * source + 1)
            )

        place = member % 4
        wanted = place ^ cross
        taps = conv_weights.reshape(3, width, width)
        tap = lax.dynamic_index_in_dim(taps, jnp.maximum(wanted - 1, 0), 0, keepdims=False)
        quarter = jnp.where(wanted == 0, skip_weights[0], tap)
        size = width // PIECES
        pieces = [[None] * PIECES for _ in range(4)]
        for n in range(PIECES):
            pieces[0][n] = move(quarter[n * size : (n + 1) * size], partner, to_x)
            pieces[2][n] = move(pieces[0][n], same, to_x)
        for n in range(PIECES):
            pieces[1][n] = move(pieces[0][n], same, to_core)
        for n in range(PIECES):
            pieces[3][n] = move(pieces[2][n], same, to_core)
        embeds = jnp.take(time_table[0], timesteps, axis=0).astype(HIGH)
        is_odd = odd == 1
        mine = jnp.where(is_odd, embeds[1:2], embeds[0:1])
        theirs = jnp.where(is_odd, embeds[0:1], embeds[1:2])
        got = move(jnp.concatenate([gains, theirs], axis=0), partner, same)
        vec = jnp.concatenate(
            [
                jnp.where(is_odd, got[:1], gains),
                jnp.where(is_odd, gains, got[:1]),
                jnp.where(is_odd, got[1:2], mine),
                jnp.where(is_odd, mine, got[1:2]),
            ],
            axis=0,
        )
        weights = call(
            gather_kernel, low(2, 4, width, width),
            where, *[p for m in pieces for p in m], skip_weights, conv_weights,
            scalars=1, limit=SMALL_BYTES,
        )
        clip = jnp.where(is_odd, clips[1].reshape(rows, width), clips[0].reshape(rows, width))
        cotan = jnp.where(
            is_odd, cotangent[1].reshape(rows, width), cotangent[0].reshape(rows, width)
        )

        one = low(rows, width)
        two = low(2 * rows, width)
        bind = lambda kernel: lambda *r: kernel(pixels, *r)
        a0, a1 = call(bind(encoder_kernel), (one, one), clip, weights, vec)
        x1 = hop(a1, 0, 1)
        a2, a3 = call(bind(encoder_kernel), (one, one), x1, weights, vec)
        x2 = hop(a3, 1, 2)
        skip = hop(a2, 1, 2)
        side = hop(after(jnp.concatenate([a0, a1], axis=0), a3), 0, pairs - 1)
        a5 = call(bind(turn_kernel), one, x2, skip, weights, vec)
        x3 = hop(a5, 2, 3)
        results = call(
            lambda *r: states_kernel(pixels, pairs, *r),
            (high(2, rows, 128), high(2, rows, width), high(2, rows, width), two, two),
            where, clip, x1, x2, x3, side, skip, weights, vec, scalars=1,
            scratch=[pltpu.VMEM((rows, width), LOW)],
        )
        states, (first_own, early_give) = results[:3], results[3:]

        d3, back_side = call(
            bind(decoder_back_kernel), (one, low(2, rows, width)), cotan, *states, weights, vec
        )
        d2 = hop(d3, 3, 2)
        g4, back_skip = call(bind(turn_back_kernel), (one, one), d2, *states, weights, vec)
        d1 = hop(g4, 2, 1)
        extra = hop(back_skip, 2, 1)
        sides = hop(after(back_side, g4), pairs - 1, 0)
        early = move(after(early_give, g4), partner, to_x)
        g2 = call(bind(encoder_back_kernel), one, d1, extra, *states, weights, vec)
        d0 = hop(g2, 1, 0)
        tall = low(2 * rows + GAIN_ROWS, width)
        own, give_late = call(
            lambda *r: last_kernel(pixels, pairs, *r), (tall, tall),
            where, cotan, d2, d1, d0, sides, after(extra, early), *states, weights, vec, scalars=1,
            scratch=[pltpu.VMEM((rows, width), HIGH)],
        )
        late = move(give_late, partner, to_x)

        chunk = 2 * width // ring + CHUNK_PAD
        steps = ring // 2
        parts = low(2 * steps, chunk, width)
        keep, give = call(
            lambda *r: weight_kernel(pixels, ring, *r), (parts, parts),
            where, own, late, first_own, early,
            scratch=[
                pltpu.VMEM((2 * ring, chunk, width), LOW),
                pltpu.VMEM((2, 2 * rows, width), LOW),
                pltpu.VMEM((4, 2 * rows, width), LOW),
            ],
            scalars=1, limit=BIG_BYTES,
        )

        def turn(i):
            ahead = -1 if i % 2 == 0 else 1
            return ((i // 4 + ahead) % ring) * 4 + i % 4

        def some(value, member_of, cores=(0, 1)):
            return lax.ppermute(
                value,
                both,
                [
                    (s * dp + i, s * dp + member_of(i))
                    for s in range(sections)
                    for i in range(dp)
                    if i % 2 in cores
                ],
            )

        first_core = member % 2 == 0
        met = some(give, to_core)
        crossed = [
            some((keep[steps + n].astype(HIGH) + met[steps + n].astype(HIGH)).astype(LOW), to_x)
            for n in range(steps)
        ]

        def item(n):
            return keep[n].astype(HIGH) + met[n].astype(HIGH) + crossed[n].astype(HIGH)

        partial = item(0).astype(LOW)
        for n in range(1, steps):
            partial = (some(partial, turn).astype(HIGH) + item(n)).astype(LOW)
        partial = jnp.where(first_core, some(partial, turn, (0,)), partial)
        part = partial + some(partial, to_core)

        mine_here = []
        across = []
        value = part
        part_across = some(part, to_x, (1,))
        for _ in range(steps - 1):
            value = some(value, turn)
            mine_here.append(value)
            across.append(some(value, to_x))
        value = some(value, turn, (0,))
        mine_here.append(jnp.where(first_core, value, part))
        last_across = some(value, to_x, (0,))
        across.append(jnp.where(first_core, last_across, part_across))
        beside = []
        for span in ((0, 1), (2,), (3,)):
            stacked = jnp.stack([v for n in span for v in (mine_here[n], across[n])])
            beside.append(some(stacked, to_core))
        return call(
            lambda *r: finish_kernel(1.0 / (count * dp), ring, *r),
            (high(1, width, width), high(1, 3 * width, width), high(1, width)),
            where, *mine_here, *across, *beside,
            scratch=[pltpu.VMEM((2 * ring, chunk, width), LOW)], scalars=1, limit=BIG_BYTES,
        )

    return local


def solution(mesh):
    placed = (
        P("dp", None, None, None),
        P("dp", None, None, None),
        P("dp"),
        P("section", None, None),
        P("section", None, None),
        P("section", None, None),
        P("section", None),
    )
    return jax.shard_map(
        make_local(dict(mesh.shape)),
        mesh=mesh,
        in_specs=placed,
        out_specs=(P("section", None, None), P("section", None, None), P("section", None)),
        check_vma=False,
    )
```

profile of v0, /device:TPU:8, one launch (start us, length us, event | category | flops | bytes accessed | tf_op | source)
XLA Modules:
  0.0 205.7 jit_solution(15348197463598722390)
XLA Ops:
  6.7 9.7 %collective-permute-done.refs_0_ = bf16[320,640]{1,0:T(8,128)(2,1)S(1)} collective-permute-done((bf16[320,640]{1,0:T(8,128)(2,1)S(1)}, bf16[320,640]{1,0:T(8,128)(2,1)S(1)}, u32[]{:S(2)}, u32[]{:S(2)}) %collective-permute-start) | collective-permute-done | bytes 409632 | tf_op jit(solution)/shard_map/ppermute | solution.py:361
  16.9 7.1 %collective-permute-done.1.refs_1_ = bf16[320,640]{1,0:T(8,128)(2,1)S(1)} collective-permute-done((bf16[320,640]{1,0:T(8,128)(2,1)}, bf16[320,640]{1,0:T(8,128)(2,1)S(1)}, u32[]{:S(2)}, u32[]{:S(2)}) %collective-permute-start.1) | collective-permute-done | bytes 409632 | tf_op jit(solution)/shard_map/ppermute | solution.py:361
  24.4 4.0 %collective-permute-start.8 = (f32[2,640]{1,0:T(2,128)S(1)}, f32[2,640]{1,0:T(2,128)S(1)}, u32[]{:S(2)}, u32[]{:S(2)}) collective-permute-start(f32[2,640]{1,0:T(2,128)S(1)} %pad_maximum_fusion.5), channel_id=1, source_target_pairs={{0,32},{1,33},{2,34},{3,35},{4,36},{5,37},{6,38},{7,39},{8,40},{9,... | collective-permute-start | bytes 15368 | tf_op jit(solution)/shard_map/ppermute | solution.py:361
  29.0 5.6 %collective-permute-done.5.refs_5_ = bf16[320,640]{1,0:T(8,128)(2,1)} collective-permute-done((bf16[320,640]{1,0:T(8,128)(2,1)S(1)}, bf16[320,640]{1,0:T(8,128)(2,1)}, u32[]{:S(2)}, u32[]{:S(2)}) %collective-permute-start.5) | collective-permute-done | bytes 409632 | tf_op jit(solution)/shard_map/ppermute | solution.py:361
  43.7 6.4 %collective-permute-done.9.r_0_.r_2_ = bf16[112,640]{1,0:T(8,128)(2,1)S(1)} collective-permute-done((bf16[112,640]{1,0:T(8,128)(2,1)S(1)}, bf16[112,640]{1,0:T(8,128)(2,1)S(1)}, u32[]{:S(2)}, u32[]{:S(2)}) %collective-permute-start.9) | collective-permute-done | bytes 143392 | tf_op jit(solution)/shard_map/ppermute | solution.py:361
  76.8 14.3 %collective-permute-done.16.r_1_.r_6_ = bf16[112,640]{1,0:T(8,128)(2,1)S(1)} collective-permute-done((bf16[112,640]{1,0:T(8,128)(2,1)S(1)}, bf16[112,640]{1,0:T(8,128)(2,1)S(1)}, u32[]{:S(2)}, u32[]{:S(2)}) %collective-permute-start.16) | collective-permute-done | bytes 143392 | tf_op jit(solution)/shard_map/ppermute | solution.py:361
  101.7 7.3 %collective-permute-done.20.r_2_ = bf16[240,640]{1,0:T(8,128)(2,1)S(1)} collective-permute-done((bf16[240,640]{1,0:T(8,128)(2,1)S(1)}, bf16[240,640]{1,0:T(8,128)(2,1)S(1)}, u32[]{:S(2)}, u32[]{:S(2)}) %collective-permute-start.20) | collective-permute-done | bytes 307232 | tf_op jit(solution)/shard_map/ppermute | solution.py:361
  112.0 3.6 %collective-permute-done.21 = bf16[8,168,640]{2,1,0:T(8,128)(2,1)S(1)} collective-permute-done((bf16[8,168,640]{2,1,0:T(8,128)(2,1)S(1)}, bf16[8,168,640]{2,1,0:T(8,128)(2,1)S(1)}, u32[]{:S(2)}, u32[]{:S(2)}) %collective-permute-start.21) | collective-permute-done | bytes 1720352 | tf_op jit(solution)/shard_map/ppermute | solution.py:472
  118.0 6.1 %collective-permute-done.22 = bf16[168,640]{1,0:T(8,128)(2,1)S(1)} collective-permute-done((bf16[168,640]{1,0:T(8,128)(2,1)S(1)}, bf16[168,640]{1,0:T(8,128)(2,1)S(1)}, u32[]{:S(2)}, u32[]{:S(2)}) %collective-permute-start.22) | collective-permute-done | bytes 215072 | tf_op jit(solution)/shard_map/ppermute | solution.py:472
  124.2 6.0 %collective-permute-start.23 = (bf16[168,640]{1,0:T(8,128)(2,1)S(1)}, bf16[168,640]{1,0:T(8,128)(2,1)S(1)}, u32[]{:S(2)}, u32[]{:S(2)}) collective-permute-start(bf16[168,640]{1,0:T(8,128)(2,1)S(1)} %fusion.6), channel_id=1, source_target_pairs={{0,28},{1,5},{2,30},{3,7},{4,0},{5,9},{6,2},{7,11},{8,4},{9,13},{1... | collective-permute-start | bytes 645128 | tf_op jit(solution)/shard_map/ppermute | solution.py:472
  130.2 3.4 %collective-permute-done.23 = bf16[168,640]{1,0:T(8,128)(2,1)S(1)} collective-permute-done((bf16[168,640]{1,0:T(8,128)(2,1)S(1)}, bf16[168,640]{1,0:T(8,128)(2,1)S(1)}, u32[]{:S(2)}, u32[]{:S(2)}) %collective-permute-start.23) | collective-permute-done | bytes 215072 | tf_op jit(solution)/shard_map/ppermute | solution.py:472
  133.7 3.8 %collective-permute-start.25 = (bf16[168,640]{1,0:T(8,128)(2,1)S(1)}, bf16[168,640]{1,0:T(8,128)(2,1)S(1)}, u32[]{:S(2)}, u32[]{:S(2)}) collective-permute-start(bf16[168,640]{1,0:T(8,128)(2,1)S(1)} %fusion.5), channel_id=1, source_target_pairs={{0,28},{1,5},{2,30},{3,7},{4,0},{5,9},{6,2},{7,11},{8,4},{9,13},{1... | collective-permute-start | bytes 645128 | tf_op jit(solution)/shard_map/ppermute | solution.py:472
  141.0 3.8 %collective-permute-start.27 = (bf16[168,640]{1,0:T(8,128)(2,1)S(1)}, bf16[168,640]{1,0:T(8,128)(2,1)S(1)}, u32[]{:S(2)}, u32[]{:S(2)}) collective-permute-start(bf16[168,640]{1,0:T(8,128)(2,1)S(1)} %fusion.3), channel_id=1, source_target_pairs={{0,28},{1,5},{2,30},{3,7},{4,0},{5,9},{6,2},{7,11},{8,4},{9,13},{1... | collective-permute-start | bytes 645128 | tf_op jit(solution)/shard_map/ppermute | solution.py:472
  144.7 3.4 %collective-permute-done.27 = bf16[168,640]{1,0:T(8,128)(2,1)S(1)} collective-permute-done((bf16[168,640]{1,0:T(8,128)(2,1)S(1)}, bf16[168,640]{1,0:T(8,128)(2,1)S(1)}, u32[]{:S(2)}, u32[]{:S(2)}) %collective-permute-start.27) | collective-permute-done | bytes 215072 | tf_op jit(solution)/shard_map/ppermute | solution.py:472
  148.3 5.6 %collective-permute-start.29 = (bf16[168,640]{1,0:T(8,128)(2,1)S(1)}, bf16[168,640]{1,0:T(8,128)(2,1)S(1)}, u32[]{:S(2)}, u32[]{:S(2)}) collective-permute-start(bf16[168,640]{1,0:T(8,128)(2,1)S(1)} %fusion.1), channel_id=1, source_target_pairs={{0,28},{2,30},{4,0},{6,2},{8,4},{10,6},{12,8},{14,10},{16,12},{18,... | collective-permute-start | bytes 645128 | tf_op jit(solution)/shard_map/ppermute | solution.py:472
  153.9 3.4 %collective-permute-done.29 = bf16[168,640]{1,0:T(8,128)(2,1)S(1)} collective-permute-done((bf16[168,640]{1,0:T(8,128)(2,1)S(1)}, bf16[168,640]{1,0:T(8,128)(2,1)S(1)}, u32[]{:S(2)}, u32[]{:S(2)}) %collective-permute-start.29) | collective-permute-done | bytes 215072 | tf_op jit(solution)/shard_map/ppermute | solution.py:472
  158.9 3.8 %collective-permute-start.31 = (bf16[168,640]{1,0:T(8,128)(2,1)S(1)}, bf16[168,640]{1,0:T(8,128)(2,1)S(1)}, u32[]{:S(2)}, u32[]{:S(2)}) collective-permute-start(bf16[168,640]{1,0:T(8,128)(2,1)S(1)} %add.113), channel_id=1, source_target_pairs={{0,28},{1,5},{2,30},{3,7},{4,0},{5,9},{6,2},{7,11},{8,4},{9,13},{1... | collective-permute-start | bytes 645128 | tf_op jit(solution)/shard_map/ppermute | solution.py:472
  162.6 3.4 %collective-permute-done.31.r_1_ = bf16[168,640]{1,0:T(8,128)(2,1)S(1)} collective-permute-done((bf16[168,640]{1,0:T(8,128)(2,1)S(1)}, bf16[168,640]{1,0:T(8,128)(2,1)S(1)}, u32[]{:S(2)}, u32[]{:S(2)}) %collective-permute-start.31) | collective-permute-done | bytes 215072 | tf_op jit(solution)/shard_map/ppermute | solution.py:472
  166.0 3.7 %collective-permute-start.32 = (bf16[168,640]{1,0:T(8,128)(2,1)S(1)}, bf16[168,640]{1,0:T(8,128)(2,1)S(1)}, u32[]{:S(2)}, u32[]{:S(2)}) collective-permute-start(bf16[168,640]{1,0:T(8,128)(2,1)S(1)} %collective-permute-done.31.r_1_), channel_id=1, source_target_pairs={{0,28},{1,5},{2,30},{3,7},{4,0},{5,9},{6,2},{7,11},{8,4},{9,13},{1... | collective-permute-start | bytes 645128 | tf_op jit(solution)/shard_map/ppermute | solution.py:472
  169.7 3.4 %collective-permute-done.32.r_2_ = bf16[168,640]{1,0:T(8,128)(2,1)S(1)} collective-permute-done((bf16[168,640]{1,0:T(8,128)(2,1)S(1)}, bf16[168,640]{1,0:T(8,128)(2,1)S(1)}, u32[]{:S(2)}, u32[]{:S(2)}) %collective-permute-start.32) | collective-permute-done | bytes 215072 | tf_op jit(solution)/shard_map/ppermute | solution.py:472
  173.1 3.7 %collective-permute-start.33 = (bf16[168,640]{1,0:T(8,128)(2,1)S(1)}, bf16[168,640]{1,0:T(8,128)(2,1)S(1)}, u32[]{:S(2)}, u32[]{:S(2)}) collective-permute-start(bf16[168,640]{1,0:T(8,128)(2,1)S(1)} %collective-permute-done.32.r_2_), channel_id=1, source_target_pairs={{0,28},{1,5},{2,30},{3,7},{4,0},{5,9},{6,2},{7,11},{8,4},{9,13},{1... | collective-permute-start | bytes 645128 | tf_op jit(solution)/shard_map/ppermute | solution.py:472
  180.9 5.6 %collective-permute-start.34 = (bf16[168,640]{1,0:T(8,128)(2,1)S(1)}, bf16[168,640]{1,0:T(8,128)(2,1)S(1)}, u32[]{:S(2)}, u32[]{:S(2)}) collective-permute-start(bf16[168,640]{1,0:T(8,128)(2,1)S(1)} %collective-permute-done.33.r_3_), channel_id=1, source_target_pairs={{0,28},{2,30},{4,0},{6,2},{8,4},{10,6},{12,8},{14,10},{16,12},{18,... | collective-permute-start | bytes 645128 | tf_op jit(solution)/shard_map/ppermute | solution.py:472
  194.0 5.6 %collective-permute-done.38 = bf16[168,640]{1,0:T(8,128)(2,1)S(1)} collective-permute-done((bf16[168,640]{1,0:T(8,128)(2,1)S(1)}, bf16[168,640]{1,0:T(8,128)(2,1)S(1)}, u32[]{:S(2)}, u32[]{:S(2)}) %collective-permute-start.38) | collective-permute-done | bytes 215072 | tf_op jit(solution)/shard_map/ppermute | solution.py:472
  201.6 4.1 %shard_map.104 = (f32[1,640,640]{2,1,0:T(8,128)}, f32[1,1920,640]{2,1,0:T(8,128)}, f32[1,640]{1,0:T(1,128)}) custom-call(s32[6]{0:T(128)S(1)} %stack.60.where_ref.r_0_, bf16[168,640]{1,0:T(8,128)(2,1)S(1)} %collective-permute-done.31.r_1_, bf16[168,640]{1,0:T(8,128)(2,1)S(1)} %collective-permute-done.32.r_2_, ...), custom_call_target="tpu_custom_call" | custom-call | tf_op jit(solution)/shard_map/pallas_call | solution.py:327
  (112 shorter events, 77.8 us)
Async XLA Ops:
  2.9 13.5 %collective-permute-start = (bf16[320,640]{1,0:T(8,128)(2,1)S(1)}, bf16[320,640]{1,0:T(8,128)(2,1)S(1)}, u32[]{:S(2)}, u32[]{:S(2)}) collective-permute-start(bf16[320,640]{1,0:T(8,128)(2,1)S(1)} %get-tuple-element.50), channel_id=1, source_target_pairs={{0,34},{1,35},{2,32},{3,33},{4,38},{5,39},{6,36},{7,37},{8,42},{9,... | collective-permute-start | bytes 1228808 | tf_op jit(solution)/shard_map/ppermute | solution.py:361
  5.9 18.2 %collective-permute-start.1 = (bf16[320,640]{1,0:T(8,128)(2,1)}, bf16[320,640]{1,0:T(8,128)(2,1)S(1)}, u32[]{:S(2)}, u32[]{:S(2)}) collective-permute-start(bf16[320,640]{1,0:T(8,128)(2,1)} %get-tuple-element.49), channel_id=1, source_target_pairs={{0,34},{1,35},{2,32},{3,33},{4,38},{5,39},{6,36},{7,37},{8,42},{9,... | collective-permute-start | bytes 1228808 | tf_op jit(solution)/shard_map/ppermute | solution.py:361
  16.4 12.6 %collective-permute-start.4 = (bf16[320,640]{1,0:T(8,128)(2,1)S(1)}, bf16[320,640]{1,0:T(8,128)(2,1)S(1)}, u32[]{:S(2)}, u32[]{:S(2)}) collective-permute-start(bf16[320,640]{1,0:T(8,128)(2,1)S(1)} %collective-permute-done.refs_0_), channel_id=1, source_target_pairs={{0,2},{1,3},{2,0},{3,1},{4,6},{5,7},{6,4},{7,5},{8,10},{9,11},{10,... | collective-permute-start | bytes 1228808 | tf_op jit(solution)/shard_map/ppermute | solution.py:361
  24.1 10.5 %collective-permute-start.5 = (bf16[320,640]{1,0:T(8,128)(2,1)S(1)}, bf16[320,640]{1,0:T(8,128)(2,1)}, u32[]{:S(2)}, u32[]{:S(2)}) collective-permute-start(bf16[320,640]{1,0:T(8,128)(2,1)S(1)} %collective-permute-done.1.refs_1_), channel_id=1, source_target_pairs={{0,2},{1,3},{2,0},{3,1},{4,6},{5,7},{6,4},{7,5},{8,10},{9,11},{10,... | collective-permute-start | bytes 1228808 | tf_op jit(solution)/shard_map/ppermute | solution.py:361
  24.4 12.0 %collective-permute-start.8 = (f32[2,640]{1,0:T(2,128)S(1)}, f32[2,640]{1,0:T(2,128)S(1)}, u32[]{:S(2)}, u32[]{:S(2)}) collective-permute-start(f32[2,640]{1,0:T(2,128)S(1)} %pad_maximum_fusion.5), channel_id=1, source_target_pairs={{0,32},{1,33},{2,34},{3,35},{4,36},{5,37},{6,38},{7,39},{8,40},{9,... | collective-permute-start | bytes 15368 | tf_op jit(solution)/shard_map/ppermute | solution.py:361
  28.5 8.0 %collective-permute-start.2 = (bf16[320,640]{1,0:T(8,128)(2,1)S(1)}, bf16[320,640]{1,0:T(8,128)(2,1)}, u32[]{:S(2)}, u32[]{:S(2)}) collective-permute-start(bf16[320,640]{1,0:T(8,128)(2,1)S(1)} %collective-permute-done.refs_0_), channel_id=1, source_target_pairs={{0,1},{1,0},{2,3},{3,2},{4,5},{5,4},{6,7},{7,6},{8,9},{9,8},{10,11... | collective-permute-start | bytes 1228808 | tf_op jit(solution)/shard_map/ppermute | solution.py:361
  28.5 8.0 %collective-permute-start.3 = (bf16[320,640]{1,0:T(8,128)(2,1)S(1)}, bf16[320,640]{1,0:T(8,128)(2,1)}, u32[]{:S(2)}, u32[]{:S(2)}) collective-permute-start(bf16[320,640]{1,0:T(8,128)(2,1)S(1)} %collective-permute-done.1.refs_1_), channel_id=1, source_target_pairs={{0,1},{1,0},{2,3},{3,2},{4,5},{5,4},{6,7},{7,6},{8,9},{9,8},{10,11... | collective-permute-start | bytes 1228808 | tf_op jit(solution)/shard_map/ppermute | solution.py:361
  70.8 20.4 %collective-permute-start.15 = (bf16[112,640]{1,0:T(8,128)(2,1)S(1)}, bf16[112,640]{1,0:T(8,128)(2,1)S(1)}, u32[]{:S(2)}, u32[]{:S(2)}) collective-permute-start(bf16[112,640]{1,0:T(8,128)(2,1)S(1)} %get-tuple-element.33), channel_id=1, source_target_pairs={{128,64},{129,65},{130,66},{131,67},{132,68},{133,69},{134,70},{13... | collective-permute-start | bytes 430088 | tf_op jit(solution)/shard_map/ppermute | solution.py:361
  72.1 23.0 %collective-permute-start.19 = (bf16[224,640]{1,0:T(8,128)(2,1)S(1)}, bf16[224,640]{1,0:T(8,128)(2,1)S(1)}, u32[]{:S(2)}, u32[]{:S(2)}) collective-permute-start(bf16[224,640]{1,0:T(8,128)(2,1)S(1)} %get-tuple-element.38), channel_id=1, source_target_pairs={{0,34},{1,35},{2,32},{3,33},{4,38},{5,39},{6,36},{7,37},{8,42},{9,... | collective-permute-start | bytes 860168 | tf_op jit(solution)/shard_map/ppermute | solution.py:361
  74.8 16.3 %collective-permute-start.16 = (bf16[112,640]{1,0:T(8,128)(2,1)S(1)}, bf16[112,640]{1,0:T(8,128)(2,1)S(1)}, u32[]{:S(2)}, u32[]{:S(2)}) collective-permute-start(bf16[112,640]{1,0:T(8,128)(2,1)S(1)} %get-tuple-element.34), channel_id=1, source_target_pairs={{128,64},{129,65},{130,66},{131,67},{132,68},{133,69},{134,70},{13... | collective-permute-start | bytes 430088 | tf_op jit(solution)/shard_map/ppermute | solution.py:361
  76.1 21.6 %collective-permute-start.18 = (bf16[2,112,640]{2,1,0:T(8,128)(2,1)S(1)}, bf16[2,112,640]{2,1,0:T(8,128)(2,1)S(1)}, u32[]{:S(2)}, u32[]{:S(2)}) collective-permute-start(bf16[2,112,640]{2,1,0:T(8,128)(2,1)S(1)} %get-tuple-element.36), channel_id=1, source_target_pairs={{192,0},{193,1},{194,2},{195,3},{196,4},{197,5},{198,6},{199,7},{2... | collective-permute-start | bytes 860168 | tf_op jit(solution)/shard_map/ppermute | solution.py:361
  100.9 8.2 %collective-permute-start.20 = (bf16[240,640]{1,0:T(8,128)(2,1)S(1)}, bf16[240,640]{1,0:T(8,128)(2,1)S(1)}, u32[]{:S(2)}, u32[]{:S(2)}) collective-permute-start(bf16[240,640]{1,0:T(8,128)(2,1)S(1)} %get-tuple-element.41), channel_id=1, source_target_pairs={{0,34},{1,35},{2,32},{3,33},{4,38},{5,39},{6,36},{7,37},{8,42},{9,... | collective-permute-start | bytes 921608 | tf_op jit(solution)/shard_map/ppermute | solution.py:361
  115.9 8.3 %collective-permute-start.22 = (bf16[168,640]{1,0:T(8,128)(2,1)S(1)}, bf16[168,640]{1,0:T(8,128)(2,1)S(1)}, u32[]{:S(2)}, u32[]{:S(2)}) collective-permute-start(bf16[168,640]{1,0:T(8,128)(2,1)S(1)} %get-tuple-element.45), channel_id=1, source_target_pairs={{0,2},{1,3},{2,0},{3,1},{4,6},{5,7},{6,4},{7,5},{8,10},{9,11},{10,... | collective-permute-start | bytes 645128 | tf_op jit(solution)/shard_map/ppermute | solution.py:472
  116.0 14.2 %collective-permute-start.24 = (bf16[168,640]{1,0:T(8,128)(2,1)S(1)}, bf16[168,640]{1,0:T(8,128)(2,1)S(1)}, u32[]{:S(2)}, u32[]{:S(2)}) collective-permute-start(bf16[168,640]{1,0:T(8,128)(2,1)S(1)} %get-tuple-element.48), channel_id=1, source_target_pairs={{0,2},{1,3},{2,0},{3,1},{4,6},{5,7},{6,4},{7,5},{8,10},{9,11},{10,... | collective-permute-start | bytes 645128 | tf_op jit(solution)/shard_map/ppermute | solution.py:472
  124.2 9.4 %collective-permute-start.23 = (bf16[168,640]{1,0:T(8,128)(2,1)S(1)}, bf16[168,640]{1,0:T(8,128)(2,1)S(1)}, u32[]{:S(2)}, u32[]{:S(2)}) collective-permute-start(bf16[168,640]{1,0:T(8,128)(2,1)S(1)} %fusion.6), channel_id=1, source_target_pairs={{0,28},{1,5},{2,30},{3,7},{4,0},{5,9},{6,2},{7,11},{8,4},{9,13},{1... | collective-permute-start | bytes 645128 | tf_op jit(solution)/shard_map/ppermute | solution.py:472
  148.3 9.0 %collective-permute-start.29 = (bf16[168,640]{1,0:T(8,128)(2,1)S(1)}, bf16[168,640]{1,0:T(8,128)(2,1)S(1)}, u32[]{:S(2)}, u32[]{:S(2)}) collective-permute-start(bf16[168,640]{1,0:T(8,128)(2,1)S(1)} %fusion.1), channel_id=1, source_target_pairs={{0,28},{2,30},{4,0},{6,2},{8,4},{10,6},{12,8},{14,10},{16,12},{18,... | collective-permute-start | bytes 645128 | tf_op jit(solution)/shard_map/ppermute | solution.py:472
  176.8 9.7 %collective-permute-start.35 = (bf16[168,640]{1,0:T(8,128)(2,1)S(1)}, bf16[168,640]{1,0:T(8,128)(2,1)S(1)}, u32[]{:S(2)}, u32[]{:S(2)}) collective-permute-start(bf16[168,640]{1,0:T(8,128)(2,1)S(1)} %collective-permute-done.31.r_1_), channel_id=1, source_target_pairs={{0,2},{1,3},{2,0},{3,1},{4,6},{5,7},{6,4},{7,5},{8,10},{9,11},{10,... | collective-permute-start | bytes 645128 | tf_op jit(solution)/shard_map/ppermute | solution.py:472
  176.8 12.6 %collective-permute-start.36 = (bf16[168,640]{1,0:T(8,128)(2,1)S(1)}, bf16[168,640]{1,0:T(8,128)(2,1)S(1)}, u32[]{:S(2)}, u32[]{:S(2)}) collective-permute-start(bf16[168,640]{1,0:T(8,128)(2,1)S(1)} %collective-permute-done.32.r_2_), channel_id=1, source_target_pairs={{0,2},{1,3},{2,0},{3,1},{4,6},{5,7},{6,4},{7,5},{8,10},{9,11},{10,... | collective-permute-start | bytes 645128 | tf_op jit(solution)/shard_map/ppermute | solution.py:472
  180.2 11.5 %collective-permute-start.37 = (bf16[168,640]{1,0:T(8,128)(2,1)S(1)}, bf16[168,640]{1,0:T(8,128)(2,1)S(1)}, u32[]{:S(2)}, u32[]{:S(2)}) collective-permute-start(bf16[168,640]{1,0:T(8,128)(2,1)S(1)} %collective-permute-done.33.r_3_), channel_id=1, source_target_pairs={{0,2},{1,3},{2,0},{3,1},{4,6},{5,7},{6,4},{7,5},{8,10},{9,11},{10,... | collective-permute-start | bytes 645128 | tf_op jit(solution)/shard_map/ppermute | solution.py:472
  180.2 13.8 %collective-permute-start.39 = (bf16[168,640]{1,0:T(8,128)(2,1)S(1)}, bf16[168,640]{1,0:T(8,128)(2,1)S(1)}, u32[]{:S(2)}, u32[]{:S(2)}) collective-permute-start(bf16[168,640]{1,0:T(8,128)(2,1)S(1)} %add.113), channel_id=1, source_target_pairs={{1,3},{3,1},{5,7},{7,5},{9,11},{11,9},{13,15},{15,13},{17,19},{19,... | collective-permute-start | bytes 645128 | tf_op jit(solution)/shard_map/ppermute | solution.py:472
  180.9 11.0 %collective-permute-start.34 = (bf16[168,640]{1,0:T(8,128)(2,1)S(1)}, bf16[168,640]{1,0:T(8,128)(2,1)S(1)}, u32[]{:S(2)}, u32[]{:S(2)}) collective-permute-start(bf16[168,640]{1,0:T(8,128)(2,1)S(1)} %collective-permute-done.33.r_3_), channel_id=1, source_target_pairs={{0,28},{2,30},{4,0},{6,2},{8,4},{10,6},{12,8},{14,10},{16,12},{18,... | collective-permute-start | bytes 645128 | tf_op jit(solution)/shard_map/ppermute | solution.py:472
  189.6 12.1 %collective-permute-start.40 = (bf16[4,168,640]{2,1,0:T(8,128)(2,1)S(1)}, bf16[4,168,640]{2,1,0:T(8,128)(2,1)S(1)}, u32[]{:S(2)}, u32[]{:S(2)}) collective-permute-start(bf16[4,168,640]{2,1,0:T(8,128)(2,1)S(1)} %pad_maximum_fusion), channel_id=1, source_target_pairs={{0,1},{1,0},{2,3},{3,2},{4,5},{5,4},{6,7},{7,6},{8,9},{9,8},{10,11... | collective-permute-start | bytes 2580488 | tf_op jit(solution)/shard_map/ppermute | solution.py:472
  191.8 8.1 %collective-permute-start.41 = (bf16[2,168,640]{2,1,0:T(8,128)(2,1)S(1)}, bf16[2,168,640]{2,1,0:T(8,128)(2,1)S(1)}, u32[]{:S(2)}, u32[]{:S(2)}) collective-permute-start(bf16[2,168,640]{2,1,0:T(8,128)(2,1)S(1)} %pad_maximum_fusion.1), channel_id=1, source_target_pairs={{0,1},{1,0},{2,3},{3,2},{4,5},{5,4},{6,7},{7,6},{8,9},{9,8},{10,11... | collective-permute-start | bytes 1290248 | tf_op jit(solution)/shard_map/ppermute | solution.py:472
  191.9 7.8 %collective-permute-start.38 = (bf16[168,640]{1,0:T(8,128)(2,1)S(1)}, bf16[168,640]{1,0:T(8,128)(2,1)S(1)}, u32[]{:S(2)}, u32[]{:S(2)}) collective-permute-start(bf16[168,640]{1,0:T(8,128)(2,1)S(1)} %collective-permute-done.34), channel_id=1, source_target_pairs={{0,2},{2,0},{4,6},{6,4},{8,10},{10,8},{12,14},{14,12},{16,18},{18,... | collective-permute-start | bytes 645128 | tf_op jit(solution)/shard_map/ppermute | solution.py:472
  (25 other events, 176.5 us)
where the time goes:
time: 209 us; the launch traced here: 206 us
  waiting for transfers between devices  103 us (49%)
  starting transfers between devices  66 us (32%)
  Pallas kernels  29 us (14%)
  other arithmetic  3.59 us (2%)
  local copies, waits for them, and re-layouts  3.2 us (2%)
    ppermute x21, waiting for transfers between devices, move(): lax.ppermute(value, both, [(s * dp + i, section_of(s) * dp + member_of(i)...  57.6 us
    ppermute x22, waiting for transfers between devices, some(): lax.ppermute(value, both, [(s * dp + i, s * dp + member_of(i)) for s in r...  45.2 us
    ppermute x22, starting transfers between devices, some(): lax.ppermute(value, both, [(s * dp + i, s * dp + member_of(i)) for s in r...  43.2 us
    pallas_call x11, Pallas kernels, call(): pl.pallas_call(kernel, out_shape=outs, in_specs=specs, scratch_shapes=scr...  29 us
    ppermute x21, starting transfers between devices, move(): lax.ppermute(value, both, [(s * dp + i, section_of(s) * dp + member_of(i)...  22.8 us
  transfers between devices with their start and end apart: 43, of which 26 were waited for; matrix products, arithmetic and copies ran while one was open for 1% of the time, Pallas kernels for 2%

commit v1 on v0

--- a/solution.py
+++ b/solution.py
@@ -12,7 +12,8 @@
 BIG_BYTES = 32 * 2**20
 CHUNK_PAD = 8
 GAIN_ROWS = 16
-PIECES = 2
+PIECES = 3
+BESIDE = ((0, 3), (3, 5))
 
 
 def dot(left, right):
@@ -246,66 +247,71 @@
     for ref in (own_ref, got_ref):
         tail = ref[2 * rows :].astype(HIGH)
         gain = gain + tail[:1] + tail[1:2]
-    grad_ref[:, used:, :] = jnp.zeros((2 * ring, CHUNK_PAD, width), LOW)
+    grad_ref[:, used:, :] = jnp.zeros((4 * ring, CHUNK_PAD, width), LOW)
     grad_ref[0, used:, :] = jnp.broadcast_to(gain, (CHUNK_PAD, width)).astype(LOW)
 
     def multiply(matrix, carry):
         value = dot_outer(left_ref[jnp.minimum(matrix, 1)], right_ref[matrix]).astype(LOW)
-        each = width // used
-        grad_ref[pl.ds(matrix * each, each), :used, :] = value.reshape(each, used, width)
+        grad_ref[pl.ds(pl.multiple_of(matrix * ring, ring), ring), :used, :] = value.reshape(
+            ring, used, width
+        )
         return carry
 
     lax.fori_loop(0, 4, multiply, 0)
     core = where_ref[0]
     z = where_ref[1]
     side = where_ref[5]
-    steps = ring // 2
-    for half in range(2):
-        first = (side ^ half) * ring
-        for n in range(steps):
-            lower = first + lax.rem(z + steps + n, ring)
-            upper = first + lax.rem(z + steps - 1 - n, ring)
-            keep_ref[half * steps + n] = grad_ref[jnp.where(core == 0, lower, upper)]
-            give_ref[half * steps + n] = grad_ref[jnp.where(core == 0, upper, lower)]
-
-
-def gather_kernel(where_ref, *refs):
-    pieces = refs[: 4 * PIECES]
-    skip_ref, conv_ref, out_ref = refs[4 * PIECES :]
+
+    def share(k, carry):
+        target = lax.rem(z + k, ring)
+        half = side ^ (k // ring)
+        keep_ref[k] = grad_ref[(core * 2 + half) * ring + target]
+        give_ref[k] = grad_ref[((1 - core) * 2 + half) * ring + target]
+        return carry
+
+    lax.fori_loop(0, 2 * ring, share, 0)
+
+
+def gather_kernel(spans, where_ref, *refs):
+    skip_ref, conv_ref, out_ref = refs[len(spans) :]
     odd = where_ref[3]
     place = where_ref[4]
+    width = skip_ref.shape[1]
+
+    def own(tap, carry):
+        start = pl.multiple_of(tap * width, width)
+        out_ref[odd, tap + 1] = conv_ref[0, pl.ds(start, width), :]
+        return carry
+
     out_ref[odd, 0] = skip_ref[0]
-    width = skip_ref.shape[1]
-    for tap in range(3):
-        out_ref[odd, tap + 1] = conv_ref[0, tap * width : (tap + 1) * width]
-    size = width // PIECES
-    for m in range(4):
-        matrix = place ^ m
-        for n in range(PIECES):
-            out_ref[1 - odd, matrix, n * size : (n + 1) * size, :] = pieces[m * PIECES + n][...]
-
-
-def finish_kernel(scale, ring, where_ref, *refs):
+    lax.fori_loop(0, 3, own, 0)
+    for ref, (m, start, stop) in zip(refs, spans):
+        out_ref[1 - odd, place ^ m, start:stop, :] = ref[...]
+
+
+def finish_kernel(scale, ring, groups, where_ref, *refs):
     skip_ref, conv_ref, gain_ref, all_ref = refs[-4:]
-    steps = ring // 2
-    own, crossed, beside = refs[:steps], refs[steps : 2 * steps], refs[2 * steps : -4]
-    chunk, width = own[0].shape
+    chunk, _ = refs[0].shape[1:]
     used = chunk - CHUNK_PAD
     core = where_ref[0]
     z = where_ref[1]
     side = where_ref[5]
-    other = [(ref, 2 * n) for ref in beside for n in range(ref.shape[0] // 2)]
-    for n in range(steps):
-        lower = lax.rem(z + 1 + n, ring)
-        upper = lax.rem(z + ring - 1 - n, ring) if n < steps - 1 else z
-        here = jnp.where(core == 0, lower, upper)
-        there = jnp.where(core == 0, upper, lower)
-        ref, at = other[n]
-        all_ref[side * ring + here] = own[n][...]
-        all_ref[(1 - side) * ring + here] = crossed[n][...]
-        all_ref[side * ring + there] = ref[at]
-        all_ref[(1 - side) * ring + there] = ref[at + 1]
-    each = width // used
+    count = len(groups)
+    own, crossed, beside = refs[:count], refs[count : 2 * count], refs[2 * count : -4]
+    other = []
+    for ref, (first, stop) in zip(beside, BESIDE):
+        at = 0
+        for g in range(first, stop):
+            other.append((ref, at))
+            at += 2 * len(groups[g])
+    for g, group in enumerate(groups):
+        ref, at = other[g]
+        for n, k in enumerate(group):
+            target = lax.rem(z + k, ring)
+            all_ref[(core * 2 + side) * ring + target] = own[g][n]
+            all_ref[(core * 2 + 1 - side) * ring + target] = crossed[g][n]
+            all_ref[((1 - core) * 2 + side) * ring + target] = ref[at + n]
+            all_ref[((1 - core) * 2 + 1 - side) * ring + target] = ref[at + len(group) + n]
 
     def place(target_ref, first):
         def step(c, carry):
@@ -315,8 +321,8 @@
 
         return step
 
-    lax.fori_loop(0, each, place(skip_ref, 0), 0)
-    lax.fori_loop(0, 3 * each, place(conv_ref, each), 0)
+    lax.fori_loop(0, ring, place(skip_ref, 0), 0)
+    lax.fori_loop(0, 3 * ring, place(conv_ref, ring), 0)
     gain_ref[...] = all_ref[0, used : used + 1, :].astype(HIGH) * scale
 
 
@@ -379,15 +385,25 @@
         taps = conv_weights.reshape(3, width, width)
         tap = lax.dynamic_index_in_dim(taps, jnp.maximum(wanted - 1, 0), 0, keepdims=False)
         quarter = jnp.where(wanted == 0, skip_weights[0], tap)
-        size = width // PIECES
-        pieces = [[None] * PIECES for _ in range(4)]
+        cuts = [(width * n // PIECES + 15) // 16 * 16 for n in range(PIECES + 1)]
+        direct = []
+        relayed = []
         for n in range(PIECES):
-            pieces[0][n] = move(quarter[n * size : (n + 1) * size], partner, to_x)
-            pieces[2][n] = move(pieces[0][n], same, to_x)
-        for n in range(PIECES):
-            pieces[1][n] = move(pieces[0][n], same, to_core)
-        for n in range(PIECES):
-            pieces[3][n] = move(pieces[2][n], same, to_core)
+            piece = move(quarter[cuts[n] : cuts[n + 1]], partner, to_x)
+            direct.append(piece)
+            relayed.append(move(piece, same, to_x))
+        spans = []
+        pieces = []
+        for m, part_list in ((0, direct), (2, relayed)):
+            for n in range(PIECES):
+                pieces.append(part_list[n])
+                spans.append((m, cuts[n], cuts[n + 1]))
+        pieces += [
+            move(jnp.concatenate(direct, axis=0), same, to_core),
+            move(jnp.concatenate(relayed[:-1], axis=0), same, to_core),
+            move(relayed[-1], same, to_core),
+        ]
+        spans += [(1, 0, width), (3, 0, cuts[-2]), (3, cuts[-2], width)]
         embeds = jnp.take(time_table[0], timesteps, axis=0).astype(HIGH)
         is_odd = odd == 1
         mine = jnp.where(is_odd, embeds[1:2], embeds[0:1])
@@ -403,8 +419,8 @@
             axis=0,
         )
         weights = call(
-            gather_kernel, low(2, 4, width, width),
-            where, *[p for m in pieces for p in m], skip_weights, conv_weights,
+            lambda *r: gather_kernel(spans, *r), low(2, 4, width, width),
+            where, *pieces, skip_weights, conv_weights,
             scalars=1, limit=SMALL_BYTES,
         )
         clip = jnp.where(is_odd, clips[1].reshape(rows, width), clips[0].reshape(rows, width))
@@ -450,73 +466,62 @@
         )
         late = move(give_late, partner, to_x)
 
-        chunk = 2 * width // ring + CHUNK_PAD
-        steps = ring // 2
-        parts = low(2 * steps, chunk, width)
+        chunk = width // ring + CHUNK_PAD
+        parts = low(2 * ring, chunk, width)
         keep, give = call(
             lambda *r: weight_kernel(pixels, ring, *r), (parts, parts),
             where, own, late, first_own, early,
             scratch=[
-                pltpu.VMEM((2 * ring, chunk, width), LOW),
+                pltpu.VMEM((4 * ring, chunk, width), LOW),
                 pltpu.VMEM((2, 2 * rows, width), LOW),
                 pltpu.VMEM((4, 2 * rows, width), LOW),
             ],
             scalars=1, limit=BIG_BYTES,
         )
-
-        def turn(i):
-            ahead = -1 if i % 2 == 0 else 1
-            return ((i // 4 + ahead) % ring) * 4 + i % 4
-
-        def some(value, member_of, cores=(0, 1)):
-            return lax.ppermute(
-                value,
-                both,
-                [
-                    (s * dp + i, s * dp + member_of(i))
-                    for s in range(sections)
-                    for i in range(dp)
-                    if i % 2 in cores
-                ],
+        down = lambda i: ((i // 4 - 1) % ring) * 4 + i % 4
+        up = lambda i: ((i // 4 + 1) % ring) * 4 + i % 4
+        met = move(give, same, to_core)
+        far = ring // 2
+        waves = [(far + n, far - 1 - n) for n in range(far)]
+        crossed = {}
+        for wave in waves:
+            out = jnp.stack(
+                [(keep[ring + k].astype(HIGH) + met[ring + k].astype(HIGH)).astype(LOW) for k in wave]
             )
-
-        first_core = member % 2 == 0
-        met = some(give, to_core)
-        crossed = [
-            some((keep[steps + n].astype(HIGH) + met[steps + n].astype(HIGH)).astype(LOW), to_x)
-            for n in range(steps)
-        ]
-
-        def item(n):
-            return keep[n].astype(HIGH) + met[n].astype(HIGH) + crossed[n].astype(HIGH)
-
-        partial = item(0).astype(LOW)
-        for n in range(1, steps):
-            partial = (some(partial, turn).astype(HIGH) + item(n)).astype(LOW)
-        partial = jnp.where(first_core, some(partial, turn, (0,)), partial)
-        part = partial + some(partial, to_core)
-
-        mine_here = []
-        across = []
-        value = part
-        part_across = some(part, to_x, (1,))
-        for _ in range(steps - 1):
-            value = some(value, turn)
-            mine_here.append(value)
-            across.append(some(value, to_x))
-        value = some(value, turn, (0,))
-        mine_here.append(jnp.where(first_core, value, part))
-        last_across = some(value, to_x, (0,))
-        across.append(jnp.where(first_core, last_across, part_across))
+            back = move(out, same, to_x)
+            for n, k in enumerate(wave):
+                crossed[k] = back[n]
+
+        def total_of(k):
+            return keep[k].astype(HIGH) + met[k].astype(HIGH) + crossed[k].astype(HIGH)
+
+        lower = move(total_of(far).astype(LOW), same, down)
+        upper = move(total_of(far - 1).astype(LOW), same, up)
+        for k in range(1, far):
+            lower = move((lower.astype(HIGH) + total_of(far + k)).astype(LOW), same, down)
+            if k < far - 1:
+                upper = move((upper.astype(HIGH) + total_of(far - 1 - k)).astype(LOW), same, up)
+        part = (total_of(0) + lower.astype(HIGH) + upper.astype(HIGH)).astype(LOW)
+        groups = [(0,)] + [(k, ring - k) for k in range(1, far)] + [(far,)]
+        lower = upper = part
+        mine_here = [part[None]]
+        across = [move(mine_here[0], same, to_x)]
+        for group in groups[1:]:
+            if len(group) > 1:
+                upper = move(upper, same, up)
+            lower = move(lower, same, down)
+            mine_here.append(jnp.stack([lower, upper][: len(group)]))
+            across.append(move(mine_here[-1], same, to_x))
         beside = []
-        for span in ((0, 1), (2,), (3,)):
-            stacked = jnp.stack([v for n in span for v in (mine_here[n], across[n])])
-            beside.append(some(stacked, to_core))
+        for first, stop in BESIDE:
+            stacked = [v for n in range(first, stop) for v in (mine_here[n], across[n])]
+            beside.append(move(jnp.concatenate(stacked, axis=0), same, to_core))
+        gathered = mine_here + across + beside
         return call(
-            lambda *r: finish_kernel(1.0 / (count * dp), ring, *r),
+            lambda *r: finish_kernel(1.0 / (count * dp), ring, groups, *r),
             (high(1, width, width), high(1, 3 * width, width), high(1, width)),
-            where, *mine_here, *across, *beside,
-            scratch=[pltpu.VMEM((2 * ring, chunk, width), LOW)], scalars=1, limit=BIG_BYTES,
+            where, *gathered,
+            scratch=[pltpu.VMEM((4 * ring, chunk, width), LOW)], scalars=1, limit=BIG_BYTES,
         )
 
     return local

time: 209 us -> 197 us (0.943)
  waiting for transfers between devices: 103 us -> 94.7 us
  starting transfers between devices: 66 us -> 60.9 us
    ppermute x22 -> x0, waiting for transfers between devices: 45.2 us -> none  [some(): lax.ppermute(value, both, [(s * dp + i, s * dp + member_of(i)) for s in r...]
    ppermute x22 -> x0, starting transfers between devices: 43.2 us -> none  [some(): lax.ppermute(value, both, [(s * dp + i, s * dp + member_of(i)) for s in r...]
    ppermute x21 -> x48, starting transfers between devices: 22.8 us -> 60.9 us  [move(): lax.ppermute(value, both, [(s * dp + i, section_of(s) * dp + member_of(i)...]
    ppermute x21 -> x48, waiting for transfers between devices: 57.6 us -> 94.7 us  [move(): lax.ppermute(value, both, [(s * dp + i, section_of(s) * dp + member_of(i)...]
  transfers between devices with their start and end apart: 43 -> 48, of which waited for: 26 -> 25; matrix products, arithmetic and copies ran while one was open for 1% -> 2% of each run, Pallas kernels for 2% -> 2%
where the time goes in v1:
time: 197 us; the launch traced here: 194 us
  waiting for transfers between devices  94.7 us (48%)
  starting transfers between devices  60.9 us (31%)
  Pallas kernels  29.1 us (15%)
  other arithmetic  4.28 us (2%)
  local copies, waits for them, and re-layouts  3.64 us (2%)
    ppermute x48, waiting for transfers between devices, move(): lax.ppermute(value, both, [(s * dp + i, section_of(s) * dp + member_of(i)...  94.7 us
    ppermute x48, starting transfers between devices, move(): lax.ppermute(value, both, [(s * dp + i, section_of(s) * dp + member_of(i)...  60.9 us
    pallas_call x11, Pallas kernels, call(): pl.pallas_call(kernel, out_shape=outs, in_specs=specs, scratch_shapes=scr...  29.1 us
  transfers between devices with their start and end apart: 48, of which 25 were waited for; matrix products, arithmetic and copies ran while one was open for 2% of the time, Pallas kernels for 2%

profile of v1, /device:TPU:8, one launch (start us, length us, event | category | flops | bytes accessed | tf_op | source)
XLA Modules:
  0.0 193.9 jit_solution(16348888321669546465)
XLA Ops:
  2.1 3.1 %collective-permute-start.2 = (bf16[208,640]{1,0:T(8,128)(2,1)S(1)}, bf16[208,640]{1,0:T(8,128)(2,1)S(1)}, u32[]{:S(2)}, u32[]{:S(2)}) collective-permute-start(bf16[208,640]{1,0:T(8,128)(2,1)S(1)} %get-tuple-element.61), channel_id=1, source_target_pairs={{0,34},{1,35},{2,32},{3,33},{4,38},{5,39},{6,36},{7,37},{8,42},{9,... | collective-permute-start | bytes 798728 | tf_op jit(solution)/shard_map/ppermute | solution.py:367
  5.4 3.1 %collective-permute-start = (bf16[224,640]{1,0:T(8,128)(2,1)S(1)}, bf16[224,640]{1,0:T(8,128)(2,1)S(1)}, u32[]{:S(2)}, u32[]{:S(2)}) collective-permute-start(bf16[224,640]{1,0:T(8,128)(2,1)S(1)} %slice_bitcast_fusion), channel_id=1, source_target_pairs={{0,34},{1,35},{2,32},{3,33},{4,38},{5,39},{6,36},{7,37},{8,42},{9,... | collective-permute-start | bytes 860168 | tf_op jit(solution)/shard_map/ppermute | solution.py:367
  9.2 9.1 %collective-permute-done.1.r_2_ = bf16[208,640]{1,0:T(8,128)(2,1)S(1)} collective-permute-done((bf16[208,640]{1,0:T(8,128)(2,1)S(1)}, bf16[208,640]{1,0:T(8,128)(2,1)S(1)}, u32[]{:S(2)}, u32[]{:S(2)}) %collective-permute-start.1) | collective-permute-done | bytes 266272 | tf_op jit(solution)/shard_map/ppermute | solution.py:367
  18.9 4.5 %collective-permute-done.r_1_ = bf16[224,640]{1,0:T(8,128)(2,1)S(1)} collective-permute-done((bf16[224,640]{1,0:T(8,128)(2,1)S(1)}, bf16[224,640]{1,0:T(8,128)(2,1)S(1)}, u32[]{:S(2)}, u32[]{:S(2)}) %collective-permute-start) | collective-permute-done | bytes 286752 | tf_op jit(solution)/shard_map/ppermute | solution.py:367
  24.6 4.0 %collective-permute-start.9 = (f32[2,640]{1,0:T(2,128)S(1)}, f32[2,640]{1,0:T(2,128)S(1)}, u32[]{:S(2)}, u32[]{:S(2)}) collective-permute-start(f32[2,640]{1,0:T(2,128)S(1)} %pad_maximum_fusion.11), channel_id=1, source_target_pairs={{0,32},{1,33},{2,34},{3,35},{4,36},{5,37},{6,38},{7,39},{8,40},{9,... | collective-permute-start | bytes 15368 | tf_op jit(solution)/shard_map/ppermute | solution.py:367
  28.7 5.4 %collective-permute-done.3.r_4_ = bf16[224,640]{1,0:T(8,128)(2,1)S(1)} collective-permute-done((bf16[224,640]{1,0:T(8,128)(2,1)S(1)}, bf16[224,640]{1,0:T(8,128)(2,1)S(1)}, u32[]{:S(2)}, u32[]{:S(2)}) %collective-permute-start.3) | collective-permute-done | bytes 286752 | tf_op jit(solution)/shard_map/ppermute | solution.py:367
  35.1 4.4 %collective-permute-done.5.r_6_ = bf16[208,640]{1,0:T(8,128)(2,1)} collective-permute-done((bf16[208,640]{1,0:T(8,128)(2,1)S(1)}, bf16[208,640]{1,0:T(8,128)(2,1)}, u32[]{:S(2)}, u32[]{:S(2)}) %collective-permute-start.5) | collective-permute-done | bytes 266272 | tf_op jit(solution)/shard_map/ppermute | solution.py:367
  49.1 6.4 %collective-permute-done.10.r_0_.r_2_ = bf16[112,640]{1,0:T(8,128)(2,1)S(1)} collective-permute-done((bf16[112,640]{1,0:T(8,128)(2,1)S(1)}, bf16[112,640]{1,0:T(8,128)(2,1)S(1)}, u32[]{:S(2)}, u32[]{:S(2)}) %collective-permute-start.10) | collective-permute-done | bytes 143392 | tf_op jit(solution)/shard_map/ppermute | solution.py:367
  79.0 2.8 %collective-permute-start.20 = (bf16[224,640]{1,0:T(8,128)(2,1)S(1)}, bf16[224,640]{1,0:T(8,128)(2,1)S(1)}, u32[]{:S(2)}, u32[]{:S(2)}) collective-permute-start(bf16[224,640]{1,0:T(8,128)(2,1)S(1)} %get-tuple-element.38), channel_id=1, source_target_pairs={{0,34},{1,35},{2,32},{3,33},{4,38},{5,39},{6,36},{7,37},{8,42},{9,... | collective-permute-start | bytes 860168 | tf_op jit(solution)/shard_map/ppermute | solution.py:367
  82.5 11.5 %collective-permute-done.17.r_1_.r_6_ = bf16[112,640]{1,0:T(8,128)(2,1)S(1)} collective-permute-done((bf16[112,640]{1,0:T(8,128)(2,1)S(1)}, bf16[112,640]{1,0:T(8,128)(2,1)S(1)}, u32[]{:S(2)}, u32[]{:S(2)}) %collective-permute-start.17) | collective-permute-done | bytes 143392 | tf_op jit(solution)/shard_map/ppermute | solution.py:367
  100.6 3.1 %shard_map.102 = (bf16[240,640]{1,0:T(8,128)(2,1)S(1)}, bf16[240,640]{1,0:T(8,128)(2,1)S(1)}) custom-call(s32[6]{0:T(128)S(1)} %stack.77.r_0_, bf16[112,640]{1,0:T(8,128)(2,1)S(1)} %select_bitcast_fusion.1.r_0_.r_1_, bf16[112,640]{1,0:T(8,128)(2,1)S(1)} %collective-permute-done.15.r_0_.r_2_, bf16[112,640]{1,0:T(8,128)(2,1)S(1)} %collective-permute-done.16.r_0_.r_3_, ...), custom_call_target="tpu_custom_call" | custom-call | tf_op jit(solution)/shard_map/pallas_call | solution.py:333
  106.6 5.3 %collective-permute-done.21.r_2_ = bf16[240,640]{1,0:T(8,128)(2,1)S(1)} collective-permute-done((bf16[240,640]{1,0:T(8,128)(2,1)S(1)}, bf16[240,640]{1,0:T(8,128)(2,1)S(1)}, u32[]{:S(2)}, u32[]{:S(2)}) %collective-permute-start.21) | collective-permute-done | bytes 307232 | tf_op jit(solution)/shard_map/ppermute | solution.py:367
  111.9 3.1 %shard_map.103 = (bf16[16,88,640]{2,1,0:T(8,128)(2,1)S(1)}, bf16[16,88,640]{2,1,0:T(8,128)(2,1)S(1)}) custom-call(s32[6]{0:T(128)S(1)} %stack.77.r_0_, bf16[240,640]{1,0:T(8,128)(2,1)S(1)} %get-tuple-element.40.r_1_, bf16[240,640]{1,0:T(8,128)(2,1)S(1)} %collective-permute-done.21.r_2_, bf16[224,640]{1,0:T(8,128)(2,1)S(1)} %get-tuple-element.42.r_3_, ...), custom_call_target="tpu_custom_call" | custom-call | tf_op jit(solution)/shard_map/pallas_call | solution.py:333
  115.1 3.7 %collective-permute-done.22 = bf16[16,88,640]{2,1,0:T(8,128)(2,1)S(1)} collective-permute-done((bf16[16,88,640]{2,1,0:T(8,128)(2,1)S(1)}, bf16[16,88,640]{2,1,0:T(8,128)(2,1)S(1)}, u32[]{:S(2)}, u32[]{:S(2)}) %collective-permute-start.22) | collective-permute-done | bytes 1802272 | tf_op jit(solution)/shard_map/ppermute | solution.py:367
  121.3 6.2 %collective-permute-done.24 = bf16[2,88,640]{2,1,0:T(8,128)(2,1)S(1)} collective-permute-done((bf16[2,88,640]{2,1,0:T(8,128)(2,1)S(1)}, bf16[2,88,640]{2,1,0:T(8,128)(2,1)S(1)}, u32[]{:S(2)}, u32[]{:S(2)}) %collective-permute-start.24) | collective-permute-done | bytes 225312 | tf_op jit(solution)/shard_map/ppermute | solution.py:367
  127.7 6.0 %collective-permute-start.25 = (bf16[88,640]{1,0:T(8,128)(2,1)S(1)}, bf16[88,640]{1,0:T(8,128)(2,1)S(1)}, u32[]{:S(2)}, u32[]{:S(2)}) collective-permute-start(bf16[88,640]{1,0:T(8,128)(2,1)S(1)} %get-tuple-element.51), channel_id=1, source_target_pairs={{0,28},{1,29},{2,30},{3,31},{4,0},{5,1},{6,2},{7,3},{8,4},{9,5},{1... | collective-permute-start | bytes 337928 | tf_op jit(solution)/shard_map/ppermute | solution.py:367
  136.0 3.6 %collective-permute-done.31 = bf16[88,640]{1,0:T(8,128)(2,1)S(1)} collective-permute-done((bf16[88,640]{1,0:T(8,128)(2,1)S(1)}, bf16[88,640]{1,0:T(8,128)(2,1)S(1)}, u32[]{:S(2)}, u32[]{:S(2)}) %collective-permute-start.31) | collective-permute-done | bytes 112672 | tf_op jit(solution)/shard_map/ppermute | solution.py:367
  148.2 2.9 %collective-permute-done.29 = bf16[88,640]{1,0:T(8,128)(2,1)S(1)} collective-permute-done((bf16[88,640]{1,0:T(8,128)(2,1)S(1)}, bf16[88,640]{1,0:T(8,128)(2,1)S(1)}, u32[]{:S(2)}, u32[]{:S(2)}) %collective-permute-start.29) | collective-permute-done | bytes 112672 | tf_op jit(solution)/shard_map/ppermute | solution.py:367
  157.0 3.0 %collective-permute-start.34 = (bf16[88,640]{1,0:T(8,128)(2,1)S(1)}, bf16[88,640]{1,0:T(8,128)(2,1)S(1)}, u32[]{:S(2)}, u32[]{:S(2)}) collective-permute-start(bf16[88,640]{1,0:T(8,128)(2,1)S(1)} %get-tuple-element.46), channel_id=1, source_target_pairs={{0,28},{1,29},{2,30},{3,31},{4,0},{5,1},{6,2},{7,3},{8,4},{9,5},{1... | collective-permute-start | bytes 337928 | tf_op jit(solution)/shard_map/ppermute | solution.py:367
  164.3 3.2 %collective-permute-start.36 = (bf16[88,640]{1,0:T(8,128)(2,1)S(1)}, bf16[88,640]{1,0:T(8,128)(2,1)S(1)}, u32[]{:S(2)}, u32[]{:S(2)}) collective-permute-start(bf16[88,640]{1,0:T(8,128)(2,1)S(1)} %collective-permute-done.34), channel_id=1, source_target_pairs={{0,28},{1,29},{2,30},{3,31},{4,0},{5,1},{6,2},{7,3},{8,4},{9,5},{1... | collective-permute-start | bytes 337928 | tf_op jit(solution)/shard_map/ppermute | solution.py:367
  170.3 3.2 %collective-permute-start.38 = (bf16[88,640]{1,0:T(8,128)(2,1)S(1)}, bf16[88,640]{1,0:T(8,128)(2,1)S(1)}, u32[]{:S(2)}, u32[]{:S(2)}) collective-permute-start(bf16[88,640]{1,0:T(8,128)(2,1)S(1)} %collective-permute-done.36), channel_id=1, source_target_pairs={{0,28},{1,29},{2,30},{3,31},{4,0},{5,1},{6,2},{7,3},{8,4},{9,5},{1... | collective-permute-start | bytes 337928 | tf_op jit(solution)/shard_map/ppermute | solution.py:367
  177.1 3.2 %collective-permute-start.40 = (bf16[88,640]{1,0:T(8,128)(2,1)S(1)}, bf16[88,640]{1,0:T(8,128)(2,1)S(1)}, u32[]{:S(2)}, u32[]{:S(2)}) collective-permute-start(bf16[88,640]{1,0:T(8,128)(2,1)S(1)} %collective-permute-done.38), channel_id=1, source_target_pairs={{0,28},{1,29},{2,30},{3,31},{4,0},{5,1},{6,2},{7,3},{8,4},{9,5},{1... | collective-permute-start | bytes 337928 | tf_op jit(solution)/shard_map/ppermute | solution.py:367
  184.3 3.2 %collective-permute-done.45.r_10_ = bf16[1,88,640]{2,1,0:T(8,128)(2,1)S(1)} collective-permute-done((bf16[1,88,640]{2,1,0:T(8,128)(2,1)S(1)}, bf16[1,88,640]{2,1,0:T(8,128)(2,1)S(1)}, u32[]{:S(2)}, u32[]{:S(2)}) %collective-permute-start.45) | collective-permute-done | bytes 112672 | tf_op jit(solution)/shard_map/ppermute | solution.py:367
  189.7 4.2 %shard_map.104 = (f32[1,640,640]{2,1,0:T(8,128)}, f32[1,1920,640]{2,1,0:T(8,128)}, f32[1,640]{1,0:T(1,128)}) custom-call(s32[6]{0:T(128)S(1)} %stack.77.r_0_, bf16[1,88,640]{2,1,0:T(8,128)(2,1)S(1)} %bitcast.68, bf16[2,88,640]{2,1,0:T(8,128)(2,1)S(1)} %pad_maximum_fusion.7.r_2_, bf16[2,88,640]{2,1,0:T(8,128)(2,1)S(1)} %pad_maximum_fusion.8.r_3_, ...), custom_call_target="tpu_custom_call" | custom-call | tf_op jit(solution)/shard_map/pallas_call | solution.py:333
  (144 shorter events, 84.1 us)
Async XLA Ops:
  2.1 16.8 %collective-permute-start.2 = (bf16[208,640]{1,0:T(8,128)(2,1)S(1)}, bf16[208,640]{1,0:T(8,128)(2,1)S(1)}, u32[]{:S(2)}, u32[]{:S(2)}) collective-permute-start(bf16[208,640]{1,0:T(8,128)(2,1)S(1)} %get-tuple-element.61), channel_id=1, source_target_pairs={{0,34},{1,35},{2,32},{3,33},{4,38},{5,39},{6,36},{7,37},{8,42},{9,... | collective-permute-start | bytes 798728 | tf_op jit(solution)/shard_map/ppermute | solution.py:367
  5.2 13.2 %collective-permute-start.1 = (bf16[208,640]{1,0:T(8,128)(2,1)S(1)}, bf16[208,640]{1,0:T(8,128)(2,1)S(1)}, u32[]{:S(2)}, u32[]{:S(2)}) collective-permute-start(bf16[208,640]{1,0:T(8,128)(2,1)S(1)} %get-tuple-element.62), channel_id=1, source_target_pairs={{0,34},{1,35},{2,32},{3,33},{4,38},{5,39},{6,36},{7,37},{8,42},{9,... | collective-permute-start | bytes 798728 | tf_op jit(solution)/shard_map/ppermute | solution.py:367
  5.4 17.9 %collective-permute-start = (bf16[224,640]{1,0:T(8,128)(2,1)S(1)}, bf16[224,640]{1,0:T(8,128)(2,1)S(1)}, u32[]{:S(2)}, u32[]{:S(2)}) collective-permute-start(bf16[224,640]{1,0:T(8,128)(2,1)S(1)} %slice_bitcast_fusion), channel_id=1, source_target_pairs={{0,34},{1,35},{2,32},{3,33},{4,38},{5,39},{6,36},{7,37},{8,42},{9,... | collective-permute-start | bytes 860168 | tf_op jit(solution)/shard_map/ppermute | solution.py:367
  18.3 10.3 %collective-permute-start.4 = (bf16[208,640]{1,0:T(8,128)(2,1)S(1)}, bf16[208,640]{1,0:T(8,128)(2,1)S(1)}, u32[]{:S(2)}, u32[]{:S(2)}) collective-permute-start(bf16[208,640]{1,0:T(8,128)(2,1)S(1)} %collective-permute-done.1.r_2_), channel_id=1, source_target_pairs={{0,2},{1,3},{2,0},{3,1},{4,6},{5,7},{6,4},{7,5},{8,10},{9,11},{10,... | collective-permute-start | bytes 798728 | tf_op jit(solution)/shard_map/ppermute | solution.py:367
  24.3 16.9 %collective-permute-start.6 = (bf16[640,640]{1,0:T(8,128)(2,1)}, bf16[640,640]{1,0:T(8,128)(2,1)}, u32[]{:S(2)}, u32[]{:S(2)}) collective-permute-start(bf16[640,640]{1,0:T(8,128)(2,1)} %pad_maximum_fusion), channel_id=1, source_target_pairs={{0,1},{1,0},{2,3},{3,2},{4,5},{5,4},{6,7},{7,6},{8,9},{9,8},{10,11... | collective-permute-start | bytes 2457608 | tf_op jit(solution)/shard_map/ppermute | solution.py:367
  24.3 9.7 %collective-permute-start.3 = (bf16[224,640]{1,0:T(8,128)(2,1)S(1)}, bf16[224,640]{1,0:T(8,128)(2,1)S(1)}, u32[]{:S(2)}, u32[]{:S(2)}) collective-permute-start(bf16[224,640]{1,0:T(8,128)(2,1)S(1)} %collective-permute-done.r_1_), channel_id=1, source_target_pairs={{0,2},{1,3},{2,0},{3,1},{4,6},{5,7},{6,4},{7,5},{8,10},{9,11},{10,... | collective-permute-start | bytes 860168 | tf_op jit(solution)/shard_map/ppermute | solution.py:367
  24.6 14.9 %collective-permute-start.9 = (f32[2,640]{1,0:T(2,128)S(1)}, f32[2,640]{1,0:T(2,128)S(1)}, u32[]{:S(2)}, u32[]{:S(2)}) collective-permute-start(f32[2,640]{1,0:T(2,128)S(1)} %pad_maximum_fusion.11), channel_id=1, source_target_pairs={{0,32},{1,33},{2,34},{3,35},{4,36},{5,37},{6,38},{7,39},{8,40},{9,... | collective-permute-start | bytes 15368 | tf_op jit(solution)/shard_map/ppermute | solution.py:367
  28.7 10.8 %collective-permute-start.5 = (bf16[208,640]{1,0:T(8,128)(2,1)S(1)}, bf16[208,640]{1,0:T(8,128)(2,1)}, u32[]{:S(2)}, u32[]{:S(2)}) collective-permute-start(bf16[208,640]{1,0:T(8,128)(2,1)S(1)} %collective-permute-done.2.r_3_), channel_id=1, source_target_pairs={{0,2},{1,3},{2,0},{3,1},{4,6},{5,7},{6,4},{7,5},{8,10},{9,11},{10,... | collective-permute-start | bytes 798728 | tf_op jit(solution)/shard_map/ppermute | solution.py:367
  47.8 7.7 %collective-permute-start.10 = (bf16[112,640]{1,0:T(8,128)(2,1)S(1)}, bf16[112,640]{1,0:T(8,128)(2,1)S(1)}, u32[]{:S(2)}, u32[]{:S(2)}) collective-permute-start(bf16[112,640]{1,0:T(8,128)(2,1)S(1)} %get-tuple-element.24), channel_id=1, source_target_pairs={{0,64},{1,65},{2,66},{3,67},{4,68},{5,69},{6,70},{7,71},{8,72},{9,... | collective-permute-start | bytes 430088 | tf_op jit(solution)/shard_map/ppermute | solution.py:367
  60.1 7.1 %collective-permute-start.14 = (bf16[224,640]{1,0:T(8,128)(2,1)S(1)}, bf16[224,640]{1,0:T(8,128)(2,1)S(1)}, u32[]{:S(2)}, u32[]{:S(2)}) collective-permute-start(bf16[224,640]{1,0:T(8,128)(2,1)S(1)} %pad_maximum_fusion.2), channel_id=1, source_target_pairs={{0,192},{1,193},{2,194},{3,195},{4,196},{5,197},{6,198},{7,199},{8... | collective-permute-start | bytes 860168 | tf_op jit(solution)/shard_map/ppermute | solution.py:367
  76.4 17.7 %collective-permute-start.16 = (bf16[112,640]{1,0:T(8,128)(2,1)S(1)}, bf16[112,640]{1,0:T(8,128)(2,1)S(1)}, u32[]{:S(2)}, u32[]{:S(2)}) collective-permute-start(bf16[112,640]{1,0:T(8,128)(2,1)S(1)} %get-tuple-element.33), channel_id=1, source_target_pairs={{128,64},{129,65},{130,66},{131,67},{132,68},{133,69},{134,70},{13... | collective-permute-start | bytes 430088 | tf_op jit(solution)/shard_map/ppermute | solution.py:367
  77.7 16.4 %collective-permute-start.17 = (bf16[112,640]{1,0:T(8,128)(2,1)S(1)}, bf16[112,640]{1,0:T(8,128)(2,1)S(1)}, u32[]{:S(2)}, u32[]{:S(2)}) collective-permute-start(bf16[112,640]{1,0:T(8,128)(2,1)S(1)} %get-tuple-element.34), channel_id=1, source_target_pairs={{128,64},{129,65},{130,66},{131,67},{132,68},{133,69},{134,70},{13... | collective-permute-start | bytes 430088 | tf_op jit(solution)/shard_map/ppermute | solution.py:367
  79.0 19.0 %collective-permute-start.20 = (bf16[224,640]{1,0:T(8,128)(2,1)S(1)}, bf16[224,640]{1,0:T(8,128)(2,1)S(1)}, u32[]{:S(2)}, u32[]{:S(2)}) collective-permute-start(bf16[224,640]{1,0:T(8,128)(2,1)S(1)} %get-tuple-element.38), channel_id=1, source_target_pairs={{0,34},{1,35},{2,32},{3,33},{4,38},{5,39},{6,36},{7,37},{8,42},{9,... | collective-permute-start | bytes 860168 | tf_op jit(solution)/shard_map/ppermute | solution.py:367
  81.8 18.8 %collective-permute-start.19 = (bf16[2,112,640]{2,1,0:T(8,128)(2,1)S(1)}, bf16[2,112,640]{2,1,0:T(8,128)(2,1)S(1)}, u32[]{:S(2)}, u32[]{:S(2)}) collective-permute-start(bf16[2,112,640]{2,1,0:T(8,128)(2,1)S(1)} %get-tuple-element.36), channel_id=1, source_target_pairs={{192,0},{193,1},{194,2},{195,3},{196,4},{197,5},{198,6},{199,7},{2... | collective-permute-start | bytes 860168 | tf_op jit(solution)/shard_map/ppermute | solution.py:367
  103.8 8.2 %collective-permute-start.21 = (bf16[240,640]{1,0:T(8,128)(2,1)S(1)}, bf16[240,640]{1,0:T(8,128)(2,1)S(1)}, u32[]{:S(2)}, u32[]{:S(2)}) collective-permute-start(bf16[240,640]{1,0:T(8,128)(2,1)S(1)} %get-tuple-element.41), channel_id=1, source_target_pairs={{0,34},{1,35},{2,32},{3,33},{4,38},{5,39},{6,36},{7,37},{8,42},{9,... | collective-permute-start | bytes 921608 | tf_op jit(solution)/shard_map/ppermute | solution.py:367
  119.1 8.5 %collective-permute-start.24 = (bf16[2,88,640]{2,1,0:T(8,128)(2,1)S(1)}, bf16[2,88,640]{2,1,0:T(8,128)(2,1)S(1)}, u32[]{:S(2)}, u32[]{:S(2)}) collective-permute-start(bf16[2,88,640]{2,1,0:T(8,128)(2,1)S(1)} %pad_maximum_fusion.4), channel_id=1, source_target_pairs={{0,2},{1,3},{2,0},{3,1},{4,6},{5,7},{6,4},{7,5},{8,10},{9,11},{10,... | collective-permute-start | bytes 675848 | tf_op jit(solution)/shard_map/ppermute | solution.py:367
  119.2 14.5 %collective-permute-start.26 = (bf16[2,88,640]{2,1,0:T(8,128)(2,1)S(1)}, bf16[2,88,640]{2,1,0:T(8,128)(2,1)S(1)}, u32[]{:S(2)}, u32[]{:S(2)}) collective-permute-start(bf16[2,88,640]{2,1,0:T(8,128)(2,1)S(1)} %pad_maximum_fusion.5), channel_id=1, source_target_pairs={{0,2},{1,3},{2,0},{3,1},{4,6},{5,7},{6,4},{7,5},{8,10},{9,11},{10,... | collective-permute-start | bytes 675848 | tf_op jit(solution)/shard_map/ppermute | solution.py:367
  127.7 8.3 %collective-permute-start.25 = (bf16[88,640]{1,0:T(8,128)(2,1)S(1)}, bf16[88,640]{1,0:T(8,128)(2,1)S(1)}, u32[]{:S(2)}, u32[]{:S(2)}) collective-permute-start(bf16[88,640]{1,0:T(8,128)(2,1)S(1)} %get-tuple-element.51), channel_id=1, source_target_pairs={{0,28},{1,29},{2,30},{3,31},{4,0},{5,1},{6,2},{7,3},{8,4},{9,5},{1... | collective-permute-start | bytes 337928 | tf_op jit(solution)/shard_map/ppermute | solution.py:367
  133.7 8.3 %collective-permute-start.28 = (bf16[2,88,640]{2,1,0:T(8,128)(2,1)S(1)}, bf16[2,88,640]{2,1,0:T(8,128)(2,1)S(1)}, u32[]{:S(2)}, u32[]{:S(2)}) collective-permute-start(bf16[2,88,640]{2,1,0:T(8,128)(2,1)S(1)} %pad_maximum_fusion.6), channel_id=1, source_target_pairs={{0,2},{1,3},{2,0},{3,1},{4,6},{5,7},{6,4},{7,5},{8,10},{9,11},{10,... | collective-permute-start | bytes 675848 | tf_op jit(solution)/shard_map/ppermute | solution.py:367
  146.1 7.2 %collective-permute-start.33 = (bf16[88,640]{1,0:T(8,128)(2,1)S(1)}, bf16[88,640]{1,0:T(8,128)(2,1)S(1)}, u32[]{:S(2)}, u32[]{:S(2)}) collective-permute-start(bf16[88,640]{1,0:T(8,128)(2,1)S(1)} %get-tuple-element.48), channel_id=1, source_target_pairs={{0,4},{1,5},{2,6},{3,7},{4,8},{5,9},{6,10},{7,11},{8,12},{9,13},{1... | collective-permute-start | bytes 337928 | tf_op jit(solution)/shard_map/ppermute | solution.py:367
  160.0 7.6 %collective-permute-start.41 = (bf16[1,88,640]{2,1,0:T(8,128)(2,1)S(1)}, bf16[1,88,640]{2,1,0:T(8,128)(2,1)S(1)}, u32[]{:S(2)}, u32[]{:S(2)}) collective-permute-start(bf16[1,88,640]{2,1,0:T(8,128)(2,1)S(1)} %bitcast.67), channel_id=1, source_target_pairs={{0,2},{1,3},{2,0},{3,1},{4,6},{5,7},{6,4},{7,5},{8,10},{9,11},{10,... | collective-permute-start | bytes 337928 | tf_op jit(solution)/shard_map/ppermute | solution.py:367
  162.9 17.5 %collective-permute-start.42 = (bf16[2,88,640]{2,1,0:T(8,128)(2,1)S(1)}, bf16[2,88,640]{2,1,0:T(8,128)(2,1)S(1)}, u32[]{:S(2)}, u32[]{:S(2)}) collective-permute-start(bf16[2,88,640]{2,1,0:T(8,128)(2,1)S(1)} %pad_maximum_fusion.7.r_2_), channel_id=1, source_target_pairs={{0,2},{1,3},{2,0},{3,1},{4,6},{5,7},{6,4},{7,5},{8,10},{9,11},{10,... | collective-permute-start | bytes 675848 | tf_op jit(solution)/shard_map/ppermute | solution.py:367
  173.6 10.4 %collective-permute-start.43 = (bf16[2,88,640]{2,1,0:T(8,128)(2,1)S(1)}, bf16[2,88,640]{2,1,0:T(8,128)(2,1)S(1)}, u32[]{:S(2)}, u32[]{:S(2)}) collective-permute-start(bf16[2,88,640]{2,1,0:T(8,128)(2,1)S(1)} %pad_maximum_fusion.8.r_3_), channel_id=1, source_target_pairs={{0,2},{1,3},{2,0},{3,1},{4,6},{5,7},{6,4},{7,5},{8,10},{9,11},{10,... | collective-permute-start | bytes 675848 | tf_op jit(solution)/shard_map/ppermute | solution.py:367
  176.3 7.8 %collective-permute-start.44 = (bf16[2,88,640]{2,1,0:T(8,128)(2,1)S(1)}, bf16[2,88,640]{2,1,0:T(8,128)(2,1)S(1)}, u32[]{:S(2)}, u32[]{:S(2)}) collective-permute-start(bf16[2,88,640]{2,1,0:T(8,128)(2,1)S(1)} %pad_maximum_fusion.9.r_4_), channel_id=1, source_target_pairs={{0,2},{1,3},{2,0},{3,1},{4,6},{5,7},{6,4},{7,5},{8,10},{9,11},{10,... | collective-permute-start | bytes 675848 | tf_op jit(solution)/shard_map/ppermute | solution.py:367
  (33 other events, 208.9 us)

commit v2 on v1

--- a/solution.py
+++ b/solution.py
@@ -272,10 +272,8 @@
     lax.fori_loop(0, 2 * ring, share, 0)
 
 
-def gather_kernel(spans, where_ref, *refs):
-    skip_ref, conv_ref, out_ref = refs[len(spans) :]
+def own_kernel(where_ref, skip_ref, conv_ref, out_ref):
     odd = where_ref[3]
-    place = where_ref[4]
     width = skip_ref.shape[1]
 
     def own(tap, carry):
@@ -285,19 +283,25 @@
 
     out_ref[odd, 0] = skip_ref[0]
     lax.fori_loop(0, 3, own, 0)
+
+
+def gather_kernel(spans, where_ref, *refs):
+    out_ref = refs[-1]
+    odd = where_ref[3]
+    place = where_ref[4]
     for ref, (m, start, stop) in zip(refs, spans):
         out_ref[1 - odd, place ^ m, start:stop, :] = ref[...]
 
 
 def finish_kernel(scale, ring, groups, where_ref, *refs):
-    skip_ref, conv_ref, gain_ref, all_ref = refs[-4:]
-    chunk, _ = refs[0].shape[1:]
+    skip_ref, conv_ref, gain_ref, all_ref, wide_ref, sem_ref = refs[-6:]
+    chunk, width = refs[0].shape[1:]
     used = chunk - CHUNK_PAD
     core = where_ref[0]
     z = where_ref[1]
     side = where_ref[5]
     count = len(groups)
-    own, crossed, beside = refs[:count], refs[count : 2 * count], refs[2 * count : -4]
+    own, crossed, beside = refs[:count], refs[count : 2 * count], refs[2 * count : -6]
     other = []
     for ref, (first, stop) in zip(beside, BESIDE):
         at = 0
@@ -313,20 +317,28 @@
             all_ref[((1 - core) * 2 + side) * ring + target] = ref[at + n]
             all_ref[((1 - core) * 2 + 1 - side) * ring + target] = ref[at + len(group) + n]
 
-    def place(target_ref, first):
+    copies = []
+    for matrix in range(4):
+
         def step(c, carry):
             start = pl.multiple_of(c * used, used)
-            target_ref[0, pl.ds(start, used), :] = all_ref[first + c, :used, :].astype(HIGH) * scale
+            value = all_ref[matrix * ring + c, :used, :].astype(HIGH) * scale
+            wide_ref[matrix, pl.ds(start, used), :] = value
             return carry
 
-        return step
-
-    lax.fori_loop(0, ring, place(skip_ref, 0), 0)
-    lax.fori_loop(0, 3 * ring, place(conv_ref, ring), 0)
+        lax.fori_loop(0, ring, step, 0)
+        if matrix == 0:
+            target = skip_ref.at[0]
+        else:
+            target = conv_ref.at[0, (matrix - 1) * width : matrix * width, :]
+        copies.append(pltpu.make_async_copy(wide_ref.at[matrix], target, sem_ref.at[matrix]))
+        copies[-1].start()
     gain_ref[...] = all_ref[0, used : used + 1, :].astype(HIGH) * scale
-
-
-def call(kernel, outs, *args, scratch=(), scalars=0, limit=SMALL_BYTES):
+    for each in copies:
+        each.wait()
+
+
+def call(kernel, outs, *args, scratch=(), scalars=0, limit=SMALL_BYTES, aliases=None, out_specs=None):
     specs = [pl.BlockSpec(memory_space=pltpu.SMEM)] * scalars + [
         pl.BlockSpec(memory_space=pltpu.VMEM)
     ] * (len(args) - scalars)
@@ -335,6 +347,8 @@
         out_shape=outs,
         in_specs=specs,
         scratch_shapes=scratch,
+        input_output_aliases=aliases or {},
+        **({} if out_specs is None else {"out_specs": out_specs}),
         compiler_params=pltpu.CompilerParams(vmem_limit_bytes=limit),
     )(*args)
 
@@ -418,9 +432,14 @@
             ],
             axis=0,
         )
+        half_weights = call(
+            own_kernel, low(2, 4, width, width), where, skip_weights, conv_weights,
+            scalars=1, out_specs=pl.BlockSpec(memory_space=pltpu.VMEM),
+        )
         weights = call(
             lambda *r: gather_kernel(spans, *r), low(2, 4, width, width),
-            where, *pieces, skip_weights, conv_weights,
+            where, *pieces, half_weights, aliases={1 + len(pieces): 0},
+            out_specs=pl.BlockSpec(memory_space=pltpu.VMEM),
             scalars=1, limit=SMALL_BYTES,
         )
         clip = jnp.where(is_odd, clips[1].reshape(rows, width), clips[0].reshape(rows, width))
@@ -521,7 +540,17 @@
             lambda *r: finish_kernel(1.0 / (count * dp), ring, groups, *r),
             (high(1, width, width), high(1, 3 * width, width), high(1, width)),
             where, *gathered,
-            scratch=[pltpu.VMEM((4 * ring, chunk, width), LOW)], scalars=1, limit=BIG_BYTES,
+            scratch=[
+                pltpu.VMEM((4 * ring, chunk, width), LOW),
+                pltpu.VMEM((4, width, width), HIGH),
+                pltpu.SemaphoreType.DMA((4,)),
+            ],
+            scalars=1, limit=BIG_BYTES,
+            out_specs=(
+                pl.BlockSpec(memory_space=pl.ANY),
+                pl.BlockSpec(memory_space=pl.ANY),
+                pl.BlockSpec(memory_space=pltpu.VMEM),
+            ),
         )
 
     return local

time: 197 us -> 200 us (1.015)
  waiting for transfers between devices: 94.7 us -> 106 us
  starting transfers between devices: 60.9 us -> 52.4 us
    ppermute x48, waiting for transfers between devices: 94.7 us -> 106 us  [move(): lax.ppermute(value, both, [(s * dp + i, section_of(s) * dp + member_of(i)...]
    ppermute x48, starting transfers between devices: 60.9 us -> 52.4 us  [move(): lax.ppermute(value, both, [(s * dp + i, section_of(s) * dp + member_of(i)...]
    pallas_call x11 -> x12, Pallas kernels: 29.1 us -> 29.8 us  [call(): pl.pallas_call(kernel, out_shape=outs, in_specs=specs, scratch_shapes=scr...]
  transfers between devices with their start and end apart: 48 -> 48, of which waited for: 25 -> 28; matrix products, arithmetic and copies ran while one was open for 2% -> 2% of each run, Pallas kernels for 2% -> 3%
where the time goes in v2:
time: 200 us; the launch traced here: 197 us
  waiting for transfers between devices  106 us (53%)
  starting transfers between devices  52.4 us (26%)
  Pallas kernels  29.8 us (15%)
  other arithmetic  4.28 us (2%)
  local copies, waits for them, and re-layouts  3.49 us (2%)
    ppermute x48, waiting for transfers between devices, move(): lax.ppermute(value, both, [(s * dp + i, section_of(s) * dp + member_of(i)...  106 us
    ppermute x48, starting transfers between devices, move(): lax.ppermute(value, both, [(s * dp + i, section_of(s) * dp + member_of(i)...  52.4 us
    pallas_call x12, Pallas kernels, call(): pl.pallas_call(kernel, out_shape=outs, in_specs=specs, scratch_shapes=scr...  29.8 us
  transfers between devices with their start and end apart: 48, of which 28 were waited for; matrix products, arithmetic and copies ran while one was open for 2% of the time, Pallas kernels for 3%

profile of v2, /device:TPU:8, one launch (start us, length us, event | category | flops | bytes accessed | tf_op | source)
XLA Modules:
  0.0 197.0 jit_solution(16412730725797623736)
XLA Ops:
  2.9 3.0 %collective-permute-start.1 = (bf16[208,640]{1,0:T(8,128)(2,1)}, bf16[208,640]{1,0:T(8,128)(2,1)S(1)}, u32[]{:S(2)}, u32[]{:S(2)}) collective-permute-start(bf16[208,640]{1,0:T(8,128)(2,1)} %get-tuple-element.62), channel_id=1, source_target_pairs={{0,34},{1,35},{2,32},{3,33},{4,38},{5,39},{6,36},{7,37},{8,42},{9,... | collective-permute-start | bytes 798728 | tf_op jit(solution)/shard_map/ppermute | solution.py:381
  6.1 3.1 %collective-permute-start = (bf16[224,640]{1,0:T(8,128)(2,1)S(1)}, bf16[224,640]{1,0:T(8,128)(2,1)S(1)}, u32[]{:S(2)}, u32[]{:S(2)}) collective-permute-start(bf16[224,640]{1,0:T(8,128)(2,1)S(1)} %slice_bitcast_fusion), channel_id=1, source_target_pairs={{0,34},{1,35},{2,32},{3,33},{4,38},{5,39},{6,36},{7,37},{8,42},{9,... | collective-permute-start | bytes 860168 | tf_op jit(solution)/shard_map/ppermute | solution.py:381
  9.9 3.6 %collective-permute-done.1.r_2_ = bf16[208,640]{1,0:T(8,128)(2,1)S(1)} collective-permute-done((bf16[208,640]{1,0:T(8,128)(2,1)}, bf16[208,640]{1,0:T(8,128)(2,1)S(1)}, u32[]{:S(2)}, u32[]{:S(2)}) %collective-permute-start.1) | collective-permute-done | bytes 266272 | tf_op jit(solution)/shard_map/ppermute | solution.py:381
  14.1 5.2 %collective-permute-done.2.r_3_ = bf16[208,640]{1,0:T(8,128)(2,1)S(1)} collective-permute-done((bf16[208,640]{1,0:T(8,128)(2,1)}, bf16[208,640]{1,0:T(8,128)(2,1)S(1)}, u32[]{:S(2)}, u32[]{:S(2)}) %collective-permute-start.2) | collective-permute-done | bytes 266272 | tf_op jit(solution)/shard_map/ppermute | solution.py:381
  19.3 5.0 %collective-permute-done.r_1_ = bf16[224,640]{1,0:T(8,128)(2,1)S(1)} collective-permute-done((bf16[224,640]{1,0:T(8,128)(2,1)S(1)}, bf16[224,640]{1,0:T(8,128)(2,1)S(1)}, u32[]{:S(2)}, u32[]{:S(2)}) %collective-permute-start) | collective-permute-done | bytes 286752 | tf_op jit(solution)/shard_map/ppermute | solution.py:381
  25.5 4.0 %collective-permute-start.9 = (f32[2,640]{1,0:T(2,128)S(1)}, f32[2,640]{1,0:T(2,128)S(1)}, u32[]{:S(2)}, u32[]{:S(2)}) collective-permute-start(f32[2,640]{1,0:T(2,128)S(1)} %pad_maximum_fusion.11), channel_id=1, source_target_pairs={{0,32},{1,33},{2,34},{3,35},{4,36},{5,37},{6,38},{7,39},{8,40},{9,... | collective-permute-start | bytes 15368 | tf_op jit(solution)/shard_map/ppermute | solution.py:381
  29.6 5.4 %collective-permute-done.3.r_4_ = bf16[224,640]{1,0:T(8,128)(2,1)S(1)} collective-permute-done((bf16[224,640]{1,0:T(8,128)(2,1)S(1)}, bf16[224,640]{1,0:T(8,128)(2,1)S(1)}, u32[]{:S(2)}, u32[]{:S(2)}) %collective-permute-start.3) | collective-permute-done | bytes 286752 | tf_op jit(solution)/shard_map/ppermute | solution.py:381
  47.1 6.4 %collective-permute-done.10.r_0_.r_2_ = bf16[112,640]{1,0:T(8,128)(2,1)S(1)} collective-permute-done((bf16[112,640]{1,0:T(8,128)(2,1)S(1)}, bf16[112,640]{1,0:T(8,128)(2,1)S(1)}, u32[]{:S(2)}, u32[]{:S(2)}) %collective-permute-start.10) | collective-permute-done | bytes 143392 | tf_op jit(solution)/shard_map/ppermute | solution.py:381
  71.6 2.8 %shard_map.101 = (bf16[112,640]{1,0:T(8,128)(2,1)S(1)}, bf16[112,640]{1,0:T(8,128)(2,1)S(1)}) custom-call(bf16[112,640]{1,0:T(8,128)(2,1)S(1)} %collective-permute-done.15.r_0_.r_2_, f32[2,112,128]{2,1,0:T(8,128)S(1)} %get-tuple-element.29.r_1_.r_2_.r_7_, f32[2,112,640]{2,1,0:T(8,128)S(1)} %get-tuple-element.30.r_2_.r_3_.r_8_, ...), custom_call_target="tpu_custom_call" | custom-call | tf_op jit(solution)/shard_map/pallas_call | solution.py:345
  75.7 2.8 %collective-permute-start.20 = (bf16[224,640]{1,0:T(8,128)(2,1)S(1)}, bf16[224,640]{1,0:T(8,128)(2,1)S(1)}, u32[]{:S(2)}, u32[]{:S(2)}) collective-permute-start(bf16[224,640]{1,0:T(8,128)(2,1)S(1)} %get-tuple-element.38), channel_id=1, source_target_pairs={{0,34},{1,35},{2,32},{3,33},{4,38},{5,39},{6,36},{7,37},{8,42},{9,... | collective-permute-start | bytes 860168 | tf_op jit(solution)/shard_map/ppermute | solution.py:381
  80.5 14.1 %collective-permute-done.17.r_1_.r_6_ = bf16[112,640]{1,0:T(8,128)(2,1)S(1)} collective-permute-done((bf16[112,640]{1,0:T(8,128)(2,1)S(1)}, bf16[112,640]{1,0:T(8,128)(2,1)S(1)}, u32[]{:S(2)}, u32[]{:S(2)}) %collective-permute-start.17) | collective-permute-done | bytes 143392 | tf_op jit(solution)/shard_map/ppermute | solution.py:381
  101.2 3.1 %shard_map.103 = (bf16[240,640]{1,0:T(8,128)(2,1)S(1)}, bf16[240,640]{1,0:T(8,128)(2,1)S(1)}) custom-call(s32[6]{0:T(128)S(1)} %stack.77.where_ref.r_0_, bf16[112,640]{1,0:T(8,128)(2,1)S(1)} %select_bitcast_fusion.1.r_0_.r_1_, bf16[112,640]{1,0:T(8,128)(2,1)S(1)} %collective-permute-done.15.r_0_.r_2_, ...), custom_call_target="tpu_custom_call" | custom-call | tf_op jit(solution)/shard_map/pallas_call | solution.py:345
  104.9 7.6 %collective-permute-done.21.r_2_ = bf16[240,640]{1,0:T(8,128)(2,1)S(1)} collective-permute-done((bf16[240,640]{1,0:T(8,128)(2,1)S(1)}, bf16[240,640]{1,0:T(8,128)(2,1)S(1)}, u32[]{:S(2)}, u32[]{:S(2)}) %collective-permute-start.21) | collective-permute-done | bytes 307232 | tf_op jit(solution)/shard_map/ppermute | solution.py:381
  112.5 3.1 %shard_map.104 = (bf16[16,88,640]{2,1,0:T(8,128)(2,1)S(1)}, bf16[16,88,640]{2,1,0:T(8,128)(2,1)S(1)}) custom-call(s32[6]{0:T(128)S(1)} %stack.77.where_ref.r_0_, bf16[240,640]{1,0:T(8,128)(2,1)S(1)} %get-tuple-element.40.r_1_, bf16[240,640]{1,0:T(8,128)(2,1)S(1)} %collective-permute-done.21.r_2_, bf16[224,640]{1,0:T(8,128)(2,1)S(1)} %get-tuple-element.42.r_3_, ...), custom_call_target="tpu_custom_call" | custom-call | tf_op jit(solution)/shard_map/pallas_call | solution.py:345
  115.7 3.7 %collective-permute-done.22 = bf16[16,88,640]{2,1,0:T(8,128)(2,1)S(1)} collective-permute-done((bf16[16,88,640]{2,1,0:T(8,128)(2,1)S(1)}, bf16[16,88,640]{2,1,0:T(8,128)(2,1)S(1)}, u32[]{:S(2)}, u32[]{:S(2)}) %collective-permute-start.22) | collective-permute-done | bytes 1802272 | tf_op jit(solution)/shard_map/ppermute | solution.py:381
  121.9 6.2 %collective-permute-done.24 = bf16[2,88,640]{2,1,0:T(8,128)(2,1)S(1)} collective-permute-done((bf16[2,88,640]{2,1,0:T(8,128)(2,1)S(1)}, bf16[2,88,640]{2,1,0:T(8,128)(2,1)S(1)}, u32[]{:S(2)}, u32[]{:S(2)}) %collective-permute-start.24) | collective-permute-done | bytes 225312 | tf_op jit(solution)/shard_map/ppermute | solution.py:381
  128.3 5.9 %collective-permute-start.25 = (bf16[88,640]{1,0:T(8,128)(2,1)S(1)}, bf16[88,640]{1,0:T(8,128)(2,1)S(1)}, u32[]{:S(2)}, u32[]{:S(2)}) collective-permute-start(bf16[88,640]{1,0:T(8,128)(2,1)S(1)} %get-tuple-element.51), channel_id=1, source_target_pairs={{0,28},{1,29},{2,30},{3,31},{4,0},{5,1},{6,2},{7,3},{8,4},{9,5},{1... | collective-permute-start | bytes 337928 | tf_op jit(solution)/shard_map/ppermute | solution.py:381
  136.6 3.6 %collective-permute-done.31 = bf16[88,640]{1,0:T(8,128)(2,1)S(1)} collective-permute-done((bf16[88,640]{1,0:T(8,128)(2,1)S(1)}, bf16[88,640]{1,0:T(8,128)(2,1)S(1)}, u32[]{:S(2)}, u32[]{:S(2)}) %collective-permute-start.31) | collective-permute-done | bytes 112672 | tf_op jit(solution)/shard_map/ppermute | solution.py:381
  148.7 2.9 %collective-permute-done.29 = bf16[88,640]{1,0:T(8,128)(2,1)S(1)} collective-permute-done((bf16[88,640]{1,0:T(8,128)(2,1)S(1)}, bf16[88,640]{1,0:T(8,128)(2,1)S(1)}, u32[]{:S(2)}, u32[]{:S(2)}) %collective-permute-start.29) | collective-permute-done | bytes 112672 | tf_op jit(solution)/shard_map/ppermute | solution.py:381
  156.7 3.7 %collective-permute-start.34 = (bf16[88,640]{1,0:T(8,128)(2,1)S(1)}, bf16[88,640]{1,0:T(8,128)(2,1)S(1)}, u32[]{:S(2)}, u32[]{:S(2)}) collective-permute-start(bf16[88,640]{1,0:T(8,128)(2,1)S(1)} %get-tuple-element.46), channel_id=1, source_target_pairs={{0,28},{1,29},{2,30},{3,31},{4,0},{5,1},{6,2},{7,3},{8,4},{9,5},{1... | collective-permute-start | bytes 337928 | tf_op jit(solution)/shard_map/ppermute | solution.py:381
  162.7 3.6 %collective-permute-done.35 = bf16[88,640]{1,0:T(8,128)(2,1)S(1)} collective-permute-done((bf16[88,640]{1,0:T(8,128)(2,1)S(1)}, bf16[88,640]{1,0:T(8,128)(2,1)S(1)}, u32[]{:S(2)}, u32[]{:S(2)}) %collective-permute-start.35) | collective-permute-done | bytes 112672 | tf_op jit(solution)/shard_map/ppermute | solution.py:381
  180.8 4.6 %collective-permute-done.40 = bf16[88,640]{1,0:T(8,128)(2,1)S(1)} collective-permute-done((bf16[88,640]{1,0:T(8,128)(2,1)S(1)}, bf16[88,640]{1,0:T(8,128)(2,1)S(1)}, u32[]{:S(2)}, u32[]{:S(2)}) %collective-permute-start.40) | collective-permute-done | bytes 112672 | tf_op jit(solution)/shard_map/ppermute | solution.py:381
  186.6 3.6 %collective-permute-done.45.r_10_ = bf16[1,88,640]{2,1,0:T(8,128)(2,1)S(1)} collective-permute-done((bf16[1,88,640]{2,1,0:T(8,128)(2,1)S(1)}, bf16[1,88,640]{2,1,0:T(8,128)(2,1)S(1)}, u32[]{:S(2)}, u32[]{:S(2)}) %collective-permute-start.45) | collective-permute-done | bytes 112672 | tf_op jit(solution)/shard_map/ppermute | solution.py:381
  192.5 4.4 %shard_map.105 = (f32[1,640,640]{2,1,0:T(8,128)}, f32[1,1920,640]{2,1,0:T(8,128)}, f32[1,640]{1,0:T(1,128)}) custom-call(s32[6]{0:T(128)S(1)} %stack.77.where_ref.r_0_, bf16[1,88,640]{2,1,0:T(8,128)(2,1)S(1)} %bitcast.68, bf16[2,88,640]{2,1,0:T(8,128)(2,1)S(1)} %pad_maximum_fusion.7.r_2_, bf16[2,88,640]{2,1,0:T(8,128)(2,1)S(1)} %pad_maximum_fusion.8.r_3_, ...), custom_call_target="tpu_custom_call" | custom-call | tf_op jit(solution)/shard_map/pallas_call | solution.py:345
  (145 shorter events, 83.8 us)
Async XLA Ops:
  2.9 10.7 %collective-permute-start.1 = (bf16[208,640]{1,0:T(8,128)(2,1)}, bf16[208,640]{1,0:T(8,128)(2,1)S(1)}, u32[]{:S(2)}, u32[]{:S(2)}) collective-permute-start(bf16[208,640]{1,0:T(8,128)(2,1)} %get-tuple-element.62), channel_id=1, source_target_pairs={{0,34},{1,35},{2,32},{3,33},{4,38},{5,39},{6,36},{7,37},{8,42},{9,... | collective-permute-start | bytes 798728 | tf_op jit(solution)/shard_map/ppermute | solution.py:381
  5.9 13.4 %collective-permute-start.2 = (bf16[208,640]{1,0:T(8,128)(2,1)}, bf16[208,640]{1,0:T(8,128)(2,1)S(1)}, u32[]{:S(2)}, u32[]{:S(2)}) collective-permute-start(bf16[208,640]{1,0:T(8,128)(2,1)} %get-tuple-element.61), channel_id=1, source_target_pairs={{0,34},{1,35},{2,32},{3,33},{4,38},{5,39},{6,36},{7,37},{8,42},{9,... | collective-permute-start | bytes 798728 | tf_op jit(solution)/shard_map/ppermute | solution.py:381
  6.1 18.1 %collective-permute-start = (bf16[224,640]{1,0:T(8,128)(2,1)S(1)}, bf16[224,640]{1,0:T(8,128)(2,1)S(1)}, u32[]{:S(2)}, u32[]{:S(2)}) collective-permute-start(bf16[224,640]{1,0:T(8,128)(2,1)S(1)} %slice_bitcast_fusion), channel_id=1, source_target_pairs={{0,34},{1,35},{2,32},{3,33},{4,38},{5,39},{6,36},{7,37},{8,42},{9,... | collective-permute-start | bytes 860168 | tf_op jit(solution)/shard_map/ppermute | solution.py:381
  13.5 16.0 %collective-permute-start.4 = (bf16[208,640]{1,0:T(8,128)(2,1)S(1)}, bf16[208,640]{1,0:T(8,128)(2,1)S(1)}, u32[]{:S(2)}, u32[]{:S(2)}) collective-permute-start(bf16[208,640]{1,0:T(8,128)(2,1)S(1)} %collective-permute-done.1.r_2_), channel_id=1, source_target_pairs={{0,2},{1,3},{2,0},{3,1},{4,6},{5,7},{6,4},{7,5},{8,10},{9,11},{10,... | collective-permute-start | bytes 798728 | tf_op jit(solution)/shard_map/ppermute | solution.py:381
  25.2 16.9 %collective-permute-start.6 = (bf16[640,640]{1,0:T(8,128)(2,1)}, bf16[640,640]{1,0:T(8,128)(2,1)}, u32[]{:S(2)}, u32[]{:S(2)}) collective-permute-start(bf16[640,640]{1,0:T(8,128)(2,1)} %pad_maximum_fusion), channel_id=1, source_target_pairs={{0,1},{1,0},{2,3},{3,2},{4,5},{5,4},{6,7},{7,6},{8,9},{9,8},{10,11... | collective-permute-start | bytes 2457608 | tf_op jit(solution)/shard_map/ppermute | solution.py:381
  25.2 9.7 %collective-permute-start.3 = (bf16[224,640]{1,0:T(8,128)(2,1)S(1)}, bf16[224,640]{1,0:T(8,128)(2,1)S(1)}, u32[]{:S(2)}, u32[]{:S(2)}) collective-permute-start(bf16[224,640]{1,0:T(8,128)(2,1)S(1)} %collective-permute-done.r_1_), channel_id=1, source_target_pairs={{0,2},{1,3},{2,0},{3,1},{4,6},{5,7},{6,4},{7,5},{8,10},{9,11},{10,... | collective-permute-start | bytes 860168 | tf_op jit(solution)/shard_map/ppermute | solution.py:381
  25.5 14.9 %collective-permute-start.9 = (f32[2,640]{1,0:T(2,128)S(1)}, f32[2,640]{1,0:T(2,128)S(1)}, u32[]{:S(2)}, u32[]{:S(2)}) collective-permute-start(f32[2,640]{1,0:T(2,128)S(1)} %pad_maximum_fusion.11), channel_id=1, source_target_pairs={{0,32},{1,33},{2,34},{3,35},{4,36},{5,37},{6,38},{7,39},{8,40},{9,... | collective-permute-start | bytes 15368 | tf_op jit(solution)/shard_map/ppermute | solution.py:381
  29.6 10.8 %collective-permute-start.5 = (bf16[208,640]{1,0:T(8,128)(2,1)S(1)}, bf16[208,640]{1,0:T(8,128)(2,1)}, u32[]{:S(2)}, u32[]{:S(2)}) collective-permute-start(bf16[208,640]{1,0:T(8,128)(2,1)S(1)} %collective-permute-done.2.r_3_), channel_id=1, source_target_pairs={{0,2},{1,3},{2,0},{3,1},{4,6},{5,7},{6,4},{7,5},{8,10},{9,11},{10,... | collective-permute-start | bytes 798728 | tf_op jit(solution)/shard_map/ppermute | solution.py:381
  45.8 7.7 %collective-permute-start.10 = (bf16[112,640]{1,0:T(8,128)(2,1)S(1)}, bf16[112,640]{1,0:T(8,128)(2,1)S(1)}, u32[]{:S(2)}, u32[]{:S(2)}) collective-permute-start(bf16[112,640]{1,0:T(8,128)(2,1)S(1)} %get-tuple-element.24), channel_id=1, source_target_pairs={{0,64},{1,65},{2,66},{3,67},{4,68},{5,69},{6,70},{7,71},{8,72},{9,... | collective-permute-start | bytes 430088 | tf_op jit(solution)/shard_map/ppermute | solution.py:381
  58.1 7.1 %collective-permute-start.14 = (bf16[224,640]{1,0:T(8,128)(2,1)S(1)}, bf16[224,640]{1,0:T(8,128)(2,1)S(1)}, u32[]{:S(2)}, u32[]{:S(2)}) collective-permute-start(bf16[224,640]{1,0:T(8,128)(2,1)S(1)} %pad_maximum_fusion.2), channel_id=1, source_target_pairs={{0,192},{1,193},{2,194},{3,195},{4,196},{5,197},{6,198},{7,199},{8... | collective-permute-start | bytes 860168 | tf_op jit(solution)/shard_map/ppermute | solution.py:381
  74.4 20.3 %collective-permute-start.16 = (bf16[112,640]{1,0:T(8,128)(2,1)S(1)}, bf16[112,640]{1,0:T(8,128)(2,1)S(1)}, u32[]{:S(2)}, u32[]{:S(2)}) collective-permute-start(bf16[112,640]{1,0:T(8,128)(2,1)S(1)} %get-tuple-element.33), channel_id=1, source_target_pairs={{128,64},{129,65},{130,66},{131,67},{132,68},{133,69},{134,70},{13... | collective-permute-start | bytes 430088 | tf_op jit(solution)/shard_map/ppermute | solution.py:381
  75.7 22.9 %collective-permute-start.20 = (bf16[224,640]{1,0:T(8,128)(2,1)S(1)}, bf16[224,640]{1,0:T(8,128)(2,1)S(1)}, u32[]{:S(2)}, u32[]{:S(2)}) collective-permute-start(bf16[224,640]{1,0:T(8,128)(2,1)S(1)} %get-tuple-element.38), channel_id=1, source_target_pairs={{0,34},{1,35},{2,32},{3,33},{4,38},{5,39},{6,36},{7,37},{8,42},{9,... | collective-permute-start | bytes 860168 | tf_op jit(solution)/shard_map/ppermute | solution.py:381
  78.5 16.1 %collective-permute-start.17 = (bf16[112,640]{1,0:T(8,128)(2,1)S(1)}, bf16[112,640]{1,0:T(8,128)(2,1)S(1)}, u32[]{:S(2)}, u32[]{:S(2)}) collective-permute-start(bf16[112,640]{1,0:T(8,128)(2,1)S(1)} %get-tuple-element.34), channel_id=1, source_target_pairs={{128,64},{129,65},{130,66},{131,67},{132,68},{133,69},{134,70},{13... | collective-permute-start | bytes 430088 | tf_op jit(solution)/shard_map/ppermute | solution.py:381
  79.8 21.4 %collective-permute-start.19 = (bf16[2,112,640]{2,1,0:T(8,128)(2,1)S(1)}, bf16[2,112,640]{2,1,0:T(8,128)(2,1)S(1)}, u32[]{:S(2)}, u32[]{:S(2)}) collective-permute-start(bf16[2,112,640]{2,1,0:T(8,128)(2,1)S(1)} %get-tuple-element.36), channel_id=1, source_target_pairs={{192,0},{193,1},{194,2},{195,3},{196,4},{197,5},{198,6},{199,7},{2... | collective-permute-start | bytes 860168 | tf_op jit(solution)/shard_map/ppermute | solution.py:381
  104.4 8.2 %collective-permute-start.21 = (bf16[240,640]{1,0:T(8,128)(2,1)S(1)}, bf16[240,640]{1,0:T(8,128)(2,1)S(1)}, u32[]{:S(2)}, u32[]{:S(2)}) collective-permute-start(bf16[240,640]{1,0:T(8,128)(2,1)S(1)} %get-tuple-element.41), channel_id=1, source_target_pairs={{0,34},{1,35},{2,32},{3,33},{4,38},{5,39},{6,36},{7,37},{8,42},{9,... | collective-permute-start | bytes 921608 | tf_op jit(solution)/shard_map/ppermute | solution.py:381
  119.7 8.5 %collective-permute-start.24 = (bf16[2,88,640]{2,1,0:T(8,128)(2,1)S(1)}, bf16[2,88,640]{2,1,0:T(8,128)(2,1)S(1)}, u32[]{:S(2)}, u32[]{:S(2)}) collective-permute-start(bf16[2,88,640]{2,1,0:T(8,128)(2,1)S(1)} %pad_maximum_fusion.4), channel_id=1, source_target_pairs={{0,2},{1,3},{2,0},{3,1},{4,6},{5,7},{6,4},{7,5},{8,10},{9,11},{10,... | collective-permute-start | bytes 675848 | tf_op jit(solution)/shard_map/ppermute | solution.py:381
  119.8 14.5 %collective-permute-start.26 = (bf16[2,88,640]{2,1,0:T(8,128)(2,1)S(1)}, bf16[2,88,640]{2,1,0:T(8,128)(2,1)S(1)}, u32[]{:S(2)}, u32[]{:S(2)}) collective-permute-start(bf16[2,88,640]{2,1,0:T(8,128)(2,1)S(1)} %pad_maximum_fusion.5), channel_id=1, source_target_pairs={{0,2},{1,3},{2,0},{3,1},{4,6},{5,7},{6,4},{7,5},{8,10},{9,11},{10,... | collective-permute-start | bytes 675848 | tf_op jit(solution)/shard_map/ppermute | solution.py:381
  128.3 8.3 %collective-permute-start.25 = (bf16[88,640]{1,0:T(8,128)(2,1)S(1)}, bf16[88,640]{1,0:T(8,128)(2,1)S(1)}, u32[]{:S(2)}, u32[]{:S(2)}) collective-permute-start(bf16[88,640]{1,0:T(8,128)(2,1)S(1)} %get-tuple-element.51), channel_id=1, source_target_pairs={{0,28},{1,29},{2,30},{3,31},{4,0},{5,1},{6,2},{7,3},{8,4},{9,5},{1... | collective-permute-start | bytes 337928 | tf_op jit(solution)/shard_map/ppermute | solution.py:381
  134.3 8.3 %collective-permute-start.28 = (bf16[2,88,640]{2,1,0:T(8,128)(2,1)S(1)}, bf16[2,88,640]{2,1,0:T(8,128)(2,1)S(1)}, u32[]{:S(2)}, u32[]{:S(2)}) collective-permute-start(bf16[2,88,640]{2,1,0:T(8,128)(2,1)S(1)} %pad_maximum_fusion.6), channel_id=1, source_target_pairs={{0,2},{1,3},{2,0},{3,1},{4,6},{5,7},{6,4},{7,5},{8,10},{9,11},{10,... | collective-permute-start | bytes 675848 | tf_op jit(solution)/shard_map/ppermute | solution.py:381
  146.7 7.2 %collective-permute-start.33 = (bf16[88,640]{1,0:T(8,128)(2,1)S(1)}, bf16[88,640]{1,0:T(8,128)(2,1)S(1)}, u32[]{:S(2)}, u32[]{:S(2)}) collective-permute-start(bf16[88,640]{1,0:T(8,128)(2,1)S(1)} %get-tuple-element.48), channel_id=1, source_target_pairs={{0,4},{1,5},{2,6},{3,7},{4,8},{5,9},{6,10},{7,11},{8,12},{9,13},{1... | collective-permute-start | bytes 337928 | tf_op jit(solution)/shard_map/ppermute | solution.py:381
  160.4 9.1 %collective-permute-start.41 = (bf16[1,88,640]{2,1,0:T(8,128)(2,1)S(1)}, bf16[1,88,640]{2,1,0:T(8,128)(2,1)S(1)}, u32[]{:S(2)}, u32[]{:S(2)}) collective-permute-start(bf16[1,88,640]{2,1,0:T(8,128)(2,1)S(1)} %bitcast.67), channel_id=1, source_target_pairs={{0,2},{1,3},{2,0},{3,1},{4,6},{5,7},{6,4},{7,5},{8,10},{9,11},{10,... | collective-permute-start | bytes 337928 | tf_op jit(solution)/shard_map/ppermute | solution.py:381
  166.4 14.3 %collective-permute-start.42 = (bf16[2,88,640]{2,1,0:T(8,128)(2,1)S(1)}, bf16[2,88,640]{2,1,0:T(8,128)(2,1)S(1)}, u32[]{:S(2)}, u32[]{:S(2)}) collective-permute-start(bf16[2,88,640]{2,1,0:T(8,128)(2,1)S(1)} %pad_maximum_fusion.7.r_2_), channel_id=1, source_target_pairs={{0,2},{1,3},{2,0},{3,1},{4,6},{5,7},{6,4},{7,5},{8,10},{9,11},{10,... | collective-permute-start | bytes 675848 | tf_op jit(solution)/shard_map/ppermute | solution.py:381
  174.3 12.2 %collective-permute-start.43 = (bf16[2,88,640]{2,1,0:T(8,128)(2,1)S(1)}, bf16[2,88,640]{2,1,0:T(8,128)(2,1)S(1)}, u32[]{:S(2)}, u32[]{:S(2)}) collective-permute-start(bf16[2,88,640]{2,1,0:T(8,128)(2,1)S(1)} %pad_maximum_fusion.8.r_3_), channel_id=1, source_target_pairs={{0,2},{1,3},{2,0},{3,1},{4,6},{5,7},{6,4},{7,5},{8,10},{9,11},{10,... | collective-permute-start | bytes 675848 | tf_op jit(solution)/shard_map/ppermute | solution.py:381
  179.4 7.1 %collective-permute-start.44 = (bf16[2,88,640]{2,1,0:T(8,128)(2,1)S(1)}, bf16[2,88,640]{2,1,0:T(8,128)(2,1)S(1)}, u32[]{:S(2)}, u32[]{:S(2)}) collective-permute-start(bf16[2,88,640]{2,1,0:T(8,128)(2,1)S(1)} %pad_maximum_fusion.9.r_4_), channel_id=1, source_target_pairs={{0,2},{1,3},{2,0},{3,1},{4,6},{5,7},{6,4},{7,5},{8,10},{9,11},{10,... | collective-permute-start | bytes 675848 | tf_op jit(solution)/shard_map/ppermute | solution.py:381
  (33 other events, 223.2 us)
